TPU v7x, 512 devices: a whole 4x8x8 slice. The times are simulated.
512 devices in a mesh: tok: 64 (over z, y), ch: 8 (over x, core).
Axes of the slice: x: 4, y: 8, z: 8, core: 2. Of those that a mesh axis runs over, the one named last changes fastest.
Arguments:
- hidden: bfloat16 [8192, 1024], P('tok'), may hold values from -13 to 13
- pre_gates: bfloat16 [2, 8192, 1024], P(None, 'tok', 'ch'), may hold values from -6 to 6
- conv_weight: bfloat16 [2, 4, 1024, 1024], P(None, None, 'tok', 'ch'), may hold values from -0.09375 to 0.09375
- head_weight: bfloat16 [1024, 20480], P('tok', 'ch'), may hold values from -8 to 8
- cluster_weight: bfloat16 [1024, 128], P('tok', 'ch'), may hold values from -0.59765625 to 0.59765625
- tail1_proj: bfloat16 [64, 1024, 256], P('tok'), may hold values from -1 to 1
- tail2_proj: bfloat16 [64, 1024, 64], P('tok'), may hold values from -1 to 1
- tail1_out: bfloat16 [64, 256, 3072], P('tok', None, 'ch'), may hold values from -12 to 12
- tail2_out: bfloat16 [64, 64, 9216], P('tok', None, 'ch'), may hold values from -30 to 30
- cluster_id: int32 [8192], P('tok'), may hold values from -1 to 127, as said below
- target: int32 [8192], P('tok'), may hold values from 0 to 20479, as said below
Outputs:
- token_loss: float32 [8192], P('tok')
- grad_input: bfloat16 [8192, 1024], P('tok', 'ch')
- proj1_grad: float32 [64, 1024, 256], P('tok', 'ch')
- proj2_grad: float32 [64, 1024, 64], P('tok', 'ch')
- out1_grad: float32 [64, 256, 3072], P('tok', None, 'ch')
- out2_grad: float32 [64, 64, 9216], P('tok', None, 'ch')
Inputs may be any that keep to these rules, and one draw needn't show every extreme that they name: `cluster_id`: in each aligned block of 128 tokens at most 2 name clusters of one owner; in every draw one owner is named by 2 tokens of every block, and every owner by 2 tokens of some block. `target`: below 20480 for a head token, below 3072 for a first-tier token, below 9216 for a second-tier token.
All inputs are finite; a program needn't handle non-finite values.
Results may differ from a plain program's by a relative error of at most 0.01.
Values may be sent and summed in bfloat16 or wider, within the bound.
No kernel may reach another device: no remote copies, remote signals or barrier semaphores. Data moves between devices by JAX's collectives and lax.ppermute only.
A program may use at most 64 MiB of HBM per device.

v0:
```python
import jax
import jax.numpy as jnp
from jax import lax
from jax.sharding import PartitionSpec as P

K = 4
LEN = 128


def merged(x, axis, combine):
    everything = jax.tree.map(lambda part: lax.all_gather(part, axis), x)
    first = jax.tree.map(lambda part: part[0], everything)

    def hop(k, so_far):
        return combine(so_far, jax.tree.map(lambda part: part[k], everything))

    return lax.fori_loop(1, lax.axis_size(axis), hop, first)


def softmax_parts(logits):
    row_max = jnp.max(logits, axis=1)
    expo_terms = jnp.exp(logits - row_max[:, None])
    return (row_max, jnp.sum(expo_terms, axis=1), expo_terms.astype(jnp.bfloat16))


def joined(left_side, right_side):
    merged_max = jnp.maximum(left_side[0], right_side[0])
    left_scale = jnp.exp(left_side[0] - merged_max)
    right_scale = jnp.exp(right_side[0] - merged_max)
    merged_sum = left_side[1] * left_scale + right_side[1] * right_scale
    if len(left_side) == 5:
        merged_value = left_side[2] * left_scale[:, None] + right_side[2] * right_scale[:, None]
        return (
            merged_max,
            merged_sum,
            merged_value,
            left_side[3] + right_side[3],
            left_side[4] + right_side[4],
        )
    return (merged_max, merged_sum, left_side[2] + right_side[2])


def joined_all(left_side, right_side):
    return tuple(
        (joined(left_group, right_group) for left_group, right_group in zip(left_side, right_side))
    )


def tier_local(features, word_ids, member, out_shard, ch_index):
    out_width = out_shard.shape[1]
    logits = jnp.dot(features, out_shard, preferred_element_type=jnp.float32)
    row_max, row_sum, weights = softmax_parts(logits)
    row_value = jnp.dot(weights, out_shard.T, preferred_element_type=jnp.float32)
    local_col = word_ids - ch_index * out_width
    inside = member & (local_col >= 0) & (local_col < out_width)
    column = jnp.clip(local_col, 0, out_width - 1)
    picked = jnp.take_along_axis(logits, column[:, None], axis=1)[:, 0]
    target_logit = jnp.where(inside, picked, 0.0)
    column_value = jnp.take(out_shard, column, axis=1).T.astype(jnp.float32)
    target_value = jnp.where(inside[:, None], column_value, 0.0)
    return (logits, inside, column, (row_max, row_sum, row_value, target_value, target_logit))


def tier_finish(features, logits, inside, column, member, totals, rows_part, proj_part):
    merged_max, merged_sum, merged_value, target_value, target_logit = totals
    log_total = merged_max + jnp.log(merged_sum)
    tail_dz = jnp.where(
        member[:, None], merged_value / merged_sum[:, None] - target_value, 0.0
    ).astype(jnp.bfloat16)
    probability = jnp.exp(logits - log_total[:, None])
    positions = jnp.arange(logits.shape[1], dtype=jnp.int32)
    target_hot = ((positions[None, :] == column[:, None]) & inside[:, None]).astype(jnp.float32)
    dlogit = jnp.where(member[:, None], probability - target_hot, 0.0).astype(jnp.bfloat16)
    out_grad = jnp.einsum("sp,sw->pw", features, dlogit, preferred_element_type=jnp.float32)
    proj_grad = jnp.einsum("sd,sp->dp", rows_part, tail_dz, preferred_element_type=jnp.float32)
    returned = jnp.einsum("sp,dp->sd", tail_dz, proj_part, preferred_element_type=jnp.float32)
    tail_loss = jnp.where(member, log_total - target_logit, 0.0)
    return (out_grad, proj_grad, returned, tail_loss)


def on_device(
    hidden,
    pre_gates,
    conv_weight,
    head_weight,
    cluster_weight,
    tail1_proj,
    tail2_proj,
    tail1_out,
    tail2_out,
    cluster_id,
    target,
):
    tokens = hidden.shape[0]
    model_width = hidden.shape[1]
    owners = lax.axis_size("tok")
    groups = lax.axis_size("ch")
    ch_index = lax.axis_index("ch")
    capacity = max(2, tokens // owners)
    narrow = model_width // groups
    col_start = ch_index * narrow
    sentinel = owners * capacity
    is_tail = cluster_id >= 0
    owner_ids = jnp.where(is_tail, cluster_id // 2, 0)
    tier_ids = jnp.where(is_tail, cluster_id % 2, -1)
    owner_range = jnp.arange(owners, dtype=jnp.int32)
    owner_hits = ((owner_ids[:, None] == owner_range[None, :]) & is_tail[:, None]).astype(jnp.int32)
    running = jnp.cumsum(owner_hits, axis=0)
    slot_ids = jnp.sum(running * owner_hits, axis=1) - 1
    flat_index = jnp.where(is_tail, owner_ids * capacity + slot_ids, sentinel)
    send_rows = (
        jnp.zeros((sentinel + 1, hidden.shape[1]), jnp.bfloat16)
        .at[flat_index]
        .set(hidden)[:sentinel]
    )
    send_meta = (
        jnp.full((sentinel + 1, 2), -1, jnp.int32)
        .at[flat_index]
        .set(jnp.stack([target, tier_ids], axis=1))[:sentinel]
    )
    got_rows, got_meta = (
        lax.all_to_all(
            send_rows.reshape(owners, capacity, -1), "tok", split_axis=0, concat_axis=0, tiled=True
        ),
        lax.all_to_all(
            send_meta.reshape(owners, capacity, 2), "tok", split_axis=0, concat_axis=0, tiled=True
        ),
    )
    conv_full, head_full, cluster_full = (
        lax.all_gather(conv_weight, "tok", axis=2, tiled=True),
        lax.all_gather(head_weight, "tok", axis=0, tiled=True),
        lax.all_gather(cluster_weight, "tok", axis=0, tiled=True),
    )
    word_logits = jnp.dot(hidden, head_full, preferred_element_type=jnp.float32)
    cluster_logits = jnp.dot(hidden, cluster_full, preferred_element_type=jnp.float32)
    head_max = jnp.maximum(jnp.max(word_logits, axis=1), jnp.max(cluster_logits, axis=1))
    word_terms = jnp.exp(word_logits - head_max[:, None])
    cluster_terms = jnp.exp(cluster_logits - head_max[:, None])
    head_sum = jnp.sum(word_terms, axis=1) + jnp.sum(cluster_terms, axis=1)
    head_value = jnp.dot(
        word_terms.astype(jnp.bfloat16), head_full.T, preferred_element_type=jnp.float32
    )
    head_value = head_value + jnp.dot(
        cluster_terms.astype(jnp.bfloat16), cluster_full.T, preferred_element_type=jnp.float32
    )
    head_words = head_full.shape[1]
    cluster_cols = cluster_full.shape[1]
    word_local = target - ch_index * head_words
    in_words = ~is_tail & (word_local >= 0) & (word_local < head_words)
    word_column = jnp.clip(word_local, 0, head_words - 1)
    cluster_local = cluster_id - ch_index * cluster_cols
    in_clusters = is_tail & (cluster_local >= 0) & (cluster_local < cluster_cols)
    cluster_column = jnp.clip(cluster_local, 0, cluster_cols - 1)
    word_pick = jnp.take_along_axis(word_logits, word_column[:, None], axis=1)[:, 0]
    cluster_pick = jnp.take_along_axis(cluster_logits, cluster_column[:, None], axis=1)[:, 0]
    head_target = jnp.where(in_words, word_pick, 0.0) + jnp.where(in_clusters, cluster_pick, 0.0)
    word_vector = jnp.take(head_full, word_column, axis=1).T.astype(jnp.float32)
    cluster_vector = jnp.take(cluster_full, cluster_column, axis=1).T.astype(jnp.float32)
    target_vector = jnp.where(in_words[:, None], word_vector, 0.0) + jnp.where(
        in_clusters[:, None], cluster_vector, 0.0
    )
    rows_in = got_rows.reshape(sentinel, -1)
    word_ids = got_meta[:, :, 0].reshape(sentinel)
    tiers = got_meta[:, :, 1].reshape(sentinel)
    first_member = tiers == 0
    second_member = tiers == 1
    first_proj = tail1_proj[0]
    second_proj = tail2_proj[0]
    first_part = lax.dynamic_slice_in_dim(first_proj, col_start, narrow, 0)
    second_part = lax.dynamic_slice_in_dim(second_proj, col_start, narrow, 0)
    rows_part = lax.dynamic_slice_in_dim(rows_in, col_start, narrow, 1)
    first_z = jnp.dot(rows_in, first_proj, preferred_element_type=jnp.float32)
    second_z = jnp.dot(rows_in, second_proj, preferred_element_type=jnp.float32)
    first_features = first_z.astype(jnp.bfloat16)
    second_features = second_z.astype(jnp.bfloat16)
    first_logits, first_inside, first_column, first_totals = tier_local(
        first_features, word_ids, first_member, tail1_out[0], ch_index
    )
    second_logits, second_inside, second_column, second_totals = tier_local(
        second_features, word_ids, second_member, tail2_out[0], ch_index
    )
    head_totals, first_totals, second_totals = merged(
        ((head_max, head_sum, head_value, target_vector, head_target), first_totals, second_totals),
        "ch",
        joined_all,
    )
    merged_max, merged_sum, merged_value, merged_vector, merged_target = head_totals
    full_grad = merged_value / merged_sum[:, None] - merged_vector
    head_grad = lax.dynamic_slice_in_dim(full_grad, col_start, narrow, 1)
    first_out_grad, first_proj_grad, first_back, first_loss = tier_finish(
        first_features,
        first_logits,
        first_inside,
        first_column,
        first_member,
        first_totals,
        rows_part,
        first_part,
    )
    second_out_grad, second_proj_grad, second_back, second_loss = tier_finish(
        second_features,
        second_logits,
        second_inside,
        second_column,
        second_member,
        second_totals,
        rows_part,
        second_part,
    )
    tail_back = first_back + second_back
    tail_loss = first_loss + second_loss
    back_rows, back_loss = (
        lax.all_to_all(
            tail_back.reshape(owners, capacity, narrow).astype(jnp.bfloat16),
            "tok",
            split_axis=0,
            concat_axis=0,
            tiled=True,
        ).astype(jnp.float32),
        lax.all_to_all(
            tail_loss.reshape(owners, capacity).astype(jnp.bfloat16),
            "tok",
            split_axis=0,
            concat_axis=0,
            tiled=True,
        ).astype(jnp.float32),
    )
    back_flat = jnp.concatenate(
        [back_rows.reshape(sentinel, narrow), jnp.zeros((1, narrow), jnp.float32)], axis=0
    )
    loss_flat = jnp.concatenate([back_loss.reshape(sentinel), jnp.zeros((1,), jnp.float32)], axis=0)
    token_loss = merged_max + jnp.log(merged_sum) - merged_target + loss_flat[flat_index]
    grad_sum = head_grad + back_flat[flat_index]
    gate_a = pre_gates[0].astype(jnp.float32)
    gate_sig = jax.nn.sigmoid(pre_gates[1].astype(jnp.float32))
    gate_grads = jnp.stack(
        [grad_sum * gate_sig, grad_sum * gate_a * gate_sig * (1.0 - gate_sig)]
    ).astype(jnp.bfloat16)
    blocks = gate_grads.reshape(2, tokens // LEN, LEN, narrow)
    shifted = jnp.stack(
        [
            jnp.pad(blocks[:, :, offset_rows:], ((0, 0), (0, 0), (0, offset_rows), (0, 0))).reshape(
                2, tokens, narrow
            )
            for offset_rows in range(K)
        ]
    )
    conv_terms = jnp.einsum("kgtc,gkrc->tr", shifted, conv_full, preferred_element_type=jnp.float32)
    conv_grad = lax.psum_scatter(
        conv_terms.astype(jnp.bfloat16), "ch", scatter_dimension=1, tiled=True
    ).astype(jnp.float32)
    grad_input = (grad_sum + conv_grad).astype(jnp.bfloat16)
    return (
        token_loss,
        grad_input,
        first_proj_grad[None],
        second_proj_grad[None],
        first_out_grad[None],
        second_out_grad[None],
    )


def solution(mesh):
    placed = (
        P("tok", None),
        P(None, "tok", "ch"),
        P(None, None, "tok", "ch"),
        P("tok", "ch"),
        P("tok", "ch"),
        P("tok", None, None),
        P("tok", None, None),
        P("tok", None, "ch"),
        P("tok", None, "ch"),
        P("tok"),
        P("tok"),
    )
    return jax.shard_map(
        on_device,
        mesh=mesh,
        in_specs=placed,
        out_specs=(
            P("tok"),
            P("tok", "ch"),
            P("tok", "ch", None),
            P("tok", "ch", None),
            P("tok", None, "ch"),
            P("tok", None, "ch"),
        ),
        check_vma=False,
    )
```

profile of v0, /device:TPU:1, one launch (start us, length us, event | category | flops | bytes accessed | tf_op | source)
XLA Modules:
  0.0 375.2 jit_solution(5379239810169169788)
XLA Ops:
  13.2 17.1 %all-to-all-start.1 = ((s32[64,2,2]{1,2,0:T(2,128)}), s32[64,2,2]{1,2,0:T(2,128)S(1)}, u32[]{:S(2)}, u32[]{:S(2)}) async-start(s32[64,2,2]{1,2,0:T(2,128)} %copy.40), calls=%async_computation.1 | async-start | bytes 131072 | tf_op jit(solution)/shard_map/all_to_all | solution.py:125
  31.4 10.0 %all-to-all-done.1 = s32[64,2,2]{1,2,0:T(2,128)S(1)} async-done(((s32[64,2,2]{1,2,0:T(2,128)}), s32[64,2,2]{1,2,0:T(2,128)S(1)}, u32[]{:S(2)}, u32[]{:S(2)}) %all-to-all-start.1) | async-done | bytes 1056 | tf_op jit(solution)/shard_map/all_to_all | solution.py:125
  47.1 4.6 %all-to-all-start = ((bf16[64,2,1024]{2,1,0:T(2,128)(2,1)}), bf16[64,2,1024]{2,1,0:T(2,128)(2,1)S(1)}, u32[]{:S(2)}, u32[]{:S(2)}) async-start(bf16[64,2,1024]{2,1,0:T(2,128)(2,1)} %reshape.612), calls=%async_computation | async-start | bytes 524288 | tf_op jit(solution)/shard_map/all_to_all | solution.py:122
  51.8 41.8 %all_gather.92 = bf16[1024,16]{1,0:T(8,128)(2,1)S(1)} all-gather(bf16[16,16]{1,0:T(8,128)(2,1)S(1)} %copy-done.20), channel_id=1, replica_groups=mesh['tok'=64,'ch'=8] {'tok'}, dimensions={0}, use_global_device_ids=true | all-gather | bytes 33280 | tf_op jit(solution)/shard_map/all_gather | solution.py:132
  98.7 6.8 %all-gather.29.cloned.1.call-done = bf16[1024,2560]{1,0:T(8,128)(2,1)} async-done(((bf16[16,2560]{1,0:T(8,128)(2,1)}), bf16[1024,2560]{1,0:T(8,128)(2,1)}) %all-gather.29.cloned.1.call-update) | async-done | bytes 5242896 | tf_op jit(solution)/shard_map/all_gather | solution.py:131
  105.5 3.4 fusion.126
  108.9 1.5 gather_fusion.6
  110.4 8.0 %copy.35 = bf16[1024,2560]{0,1:T(8,128)(2,1)} copy(bf16[1024,2560]{1,0:T(8,128)(2,1)} %all-gather.29.cloned.1.call-done) | data formatting | bytes 10485760 | tf_op jit(solution)/shard_map/all_gather | solution.py:131
  118.3 4.2 %gather_fusion = bf16[128,1024]{1,0:T(8,128)(2,1)S(1)} fusion(bf16[1024,2560]{0,1:T(8,128)(2,1)} %copy.35, s32[1024]{0:T(1024)S(1)} %pad_clamp_fusion.4), kind=kCustom, calls=%fused_computation | custom fusion | bytes 524800 | tf_op jit(solution)/shard_map/jit(_take)/gather | solution.py:157
  124.5 4.4 %fusion.28 = f32[128,1024]{1,0:T(8,128)S(1)} fusion(bf16[1024,2560]{1,0:T(8,128)(2,1)} %all-gather.29.cloned.1.call-done, f32[128,2560]{1,0:T(8,128)S(1)} %get-tuple-element.948, f32[128]{0:T(128)S(1)} %max.57), kind=kOutput, calls=%fused_computation.71 | convolution fusion | flops 671744000 | bytes 7078400 | tf_op jit(solution)/shard_map/dot_general | solution.py:140
  133.4 18.3 %all-gather.12 = f32[1024,64]{1,0:T(8,128)S(1)} all-gather(f32[128,64]{1,0:T(8,128)S(1)} %convert_select_fusion.1), channel_id=14, replica_groups=mesh['tok'=64,'ch'=8] {'ch'}, dimensions={0}, use_global_device_ids=true | all-gather | bytes 294912 | tf_op jit(solution)/shard_map/all_gather | solution.py:11
  153.6 12.9 %all-gather.11 = f32[1024,64]{0,1:T(8,128)S(1)} all-gather(f32[128,64]{0,1:T(8,128)S(1)} %fusion.35), channel_id=13, replica_groups=mesh['tok'=64,'ch'=8] {'ch'}, dimensions={0}, use_global_device_ids=true | all-gather | bytes 294912 | tf_op jit(solution)/shard_map/all_gather | solution.py:11
  168.0 1.5 gather_fusion.9
  169.5 10.0 %all-gather.21 = f32[8,1,128]{2,1,0:T(1,128)S(1)} all-gather(f32[1,1,128]{2,1,0:T(1,128)S(1)} %fusion.115), channel_id=1, replica_groups=mesh['tok'=64,'ch'=8] {'ch'}, dimensions={0}, use_global_device_ids=true | all-gather | bytes 4608 | tf_op jit(solution)/shard_map/all_gather | solution.py:11
  179.5 1.5 gather_fusion.8
  181.0 8.1 %all-gather.18 = f32[8,1,128]{2,1,0:T(1,128)S(1)} all-gather(f32[1,1,128]{2,1,0:T(1,128)S(1)} %fusion.116), channel_id=1, replica_groups=mesh['tok'=64,'ch'=8] {'ch'}, dimensions={0}, use_global_device_ids=true | all-gather | bytes 4608 | tf_op jit(solution)/shard_map/all_gather | solution.py:11
  189.2 9.8 %all-gather.20 = f32[8,1,128]{2,1,0:T(1,128)S(1)} all-gather(f32[1,1,128]{2,1,0:T(1,128)S(1)} %bitcast.298), channel_id=12, replica_groups=mesh['tok'=64,'ch'=8] {'ch'}, dimensions={0}, use_global_device_ids=true | all-gather | bytes 4608 | tf_op jit(solution)/shard_map/all_gather | solution.py:11
  199.0 8.3 %all-gather.17 = f32[8,1,128]{2,1,0:T(1,128)S(1)} all-gather(f32[1,1,128]{2,1,0:T(1,128)S(1)} %bitcast.297), channel_id=8, replica_groups=mesh['tok'=64,'ch'=8] {'ch'}, dimensions={0}, use_global_device_ids=true | all-gather | bytes 4608 | tf_op jit(solution)/shard_map/all_gather | solution.py:11
  207.3 9.5 %all-gather.19 = f32[8,1,128]{2,1,0:T(1,128)S(1)} all-gather(f32[1,1,128]{2,1,0:T(1,128)S(1)} %bitcast.295), channel_id=11, replica_groups=mesh['tok'=64,'ch'=8] {'ch'}, dimensions={0}, use_global_device_ids=true | all-gather | bytes 4608 | tf_op jit(solution)/shard_map/all_gather | solution.py:11
  216.8 8.2 %all-gather.16 = f32[8,1,128]{2,1,0:T(1,128)S(1)} all-gather(f32[1,1,128]{2,1,0:T(1,128)} %bitcast.294), channel_id=7, replica_groups=mesh['tok'=64,'ch'=8] {'ch'}, dimensions={0}, use_global_device_ids=true | all-gather | bytes 4608 | tf_op jit(solution)/shard_map/all_gather | solution.py:11
  227.3 9.7 %all-gather.15 = f32[8,1,128]{2,1,0:T(1,128)S(1)} all-gather(f32[1,1,128]{2,1,0:T(1,128)S(1)} %copy-done.28), channel_id=6, replica_groups=mesh['tok'=64,'ch'=8] {'ch'}, dimensions={0}, use_global_device_ids=true | all-gather | bytes 4608 | tf_op jit(solution)/shard_map/all_gather | solution.py:11
  236.9 8.5 %all-gather.14 = f32[8,1,128]{2,1,0:T(1,128)S(1)} all-gather(f32[1,1,128]{2,1,0:T(1,128)S(1)} %add_bitcast_fusion.1), channel_id=3, replica_groups=mesh['tok'=64,'ch'=8] {'ch'}, dimensions={0}, use_global_device_ids=true | all-gather | bytes 4608 | tf_op jit(solution)/shard_map/all_gather | solution.py:11
  245.4 9.4 %all-gather.13 = f32[8,1,128]{2,1,0:T(1,128)S(1)} all-gather(f32[1,1,128]{2,1,0:T(1,128)S(1)} %bitcast.282), channel_id=2, replica_groups=mesh['tok'=64,'ch'=8] {'ch'}, dimensions={0}, use_global_device_ids=true | all-gather | bytes 4608 | tf_op jit(solution)/shard_map/all_gather | solution.py:11
  257.0 25.8 %while.43 = (s32[]{:T(128)}, f32[128]{0:T(128)S(1)}, f32[128]{0:T(128)S(1)}, f32[128,1024]{1,0:T(8,128)S(1)}, f32[128,1024]{1,0:T(8,128)S(1)}, /*index=5*/f32[12...) while((s32[]{:T(128)}, f32[128]{0:T(128)S(1)}, ...), condition=%wide.region_13.14_spmd, body=%wide.region_12.13_spmd.sunk | while | flops 690821 | bytes 4149103 | solution.py:17
  271.8 1.5 bitcast_add_fusion.6
  283.3 1.5 fusion.27
  284.8 9.9 %all-to-all-start.3 = ((bf16[64,2,128]{2,1,0:T(2,128)(2,1)}), bf16[64,2,128]{2,1,0:T(2,128)(2,1)S(1)}, u32[]{:S(2)}, u32[]{:S(2)}) async-start(bf16[64,2,128]{2,1,0:T(2,128)(2,1)} %bitcast.71), calls=%async_computation.3 | async-start | bytes 65536 | tf_op jit(solution)/shard_map/all_to_all | solution.py:213
  297.7 7.8 %all-to-all-done.3 = bf16[64,2,128]{2,1,0:T(2,128)(2,1)S(1)} async-done(((bf16[64,2,128]{2,1,0:T(2,128)(2,1)}), bf16[64,2,128]{2,1,0:T(2,128)(2,1)S(1)}, u32[]{:S(2)}, u32[]{:S(2)}) %all-to-all-start.3) | async-done | bytes 32800 | tf_op jit(solution)/shard_map/all_to_all | solution.py:213
  305.5 4.6 %all-to-all-start.2 = ((bf16[64,1,2]{2,1,0:T(2,128)(2,1)}), bf16[64,1,2]{2,1,0:T(2,128)(2,1)S(1)}, u32[]{:S(2)}, u32[]{:S(2)}) async-start(bf16[64,1,2]{2,1,0:T(2,128)(2,1)} %convert_element_type.153), calls=%async_computation.2 | async-start | bytes 65536 | tf_op jit(solution)/shard_map/all_to_all | solution.py:220
  311.2 17.7 %all-gather.31.cloned.1.call-done = bf16[2,4,1024,128]{3,2,1,0:T(8,128)(2,1)} async-done(((bf16[2,4,16,128]{3,2,1,0:T(8,128)(2,1)}), bf16[2,4,1024,128]{3,2,1,0:T(8,128)(2,1)}) %all-gather.31.cloned.1.call-update) | async-done | bytes 2097168 | tf_op jit(solution)/shard_map/all_gather | solution.py:130
  328.8 2.4 fusion.24
  336.0 30.9 %reduce-scatter.4.cloned.1.call-done = bf16[128,128]{1,0:T(8,128)(2,1)} async-done(((bf16[1024,128]{1,0:T(8,128)(2,1)}), bf16[128,128]{1,0:T(8,128)(2,1)}) %reduce-scatter.4.cloned.1.call-update) | async-done | bytes 32784
  (254 shorter events, 66.5 us)
Async XLA Ops:
  7.2 88.1 %copy-start = (bf16[1,1024,256]{2,1,0:T(8,128)(2,1)S(1)}, bf16[1,1024,256]{2,1,0:T(8,128)(2,1)}, u32[]{:S(2)}) copy-start(bf16[1,1024,256]{2,1,0:T(8,128)(2,1)} %param.18) | copy-start | bytes 1572868
  7.2 37.9 %copy-start.4 = (bf16[128,1024]{1,0:T(8,128)(2,1)S(1)}, bf16[128,1024]{1,0:T(8,128)(2,1)}, u32[]{:S(2)}) copy-start(bf16[128,1024]{1,0:T(8,128)(2,1)} %param.13) | copy-start | bytes 786436
  7.2 98.3 %all-gather.29.cloned.1.call-start = ((), (), s32[]{:S(2)}) async-start(), calls=%async_computation.5 | async-start | bytes 5324800 | tf_op jit(solution)/shard_map/all_gather | solution.py:131
  9.7 42.1 %copy-start.20 = (bf16[16,16]{1,0:T(8,128)(2,1)S(1)}, bf16[16,16]{1,0:T(8,128)(2,1)}, u32[]{:S(2)}) copy-start(bf16[16,16]{1,0:T(8,128)(2,1)} %param.17) | copy-start | bytes 1540
  10.4 83.2 %copy-start.26 = (s32[128]{0:T(128)}, s32[128]{0:T(128)S(1)}, u32[]{:S(2)}) copy-start(s32[128]{0:T(128)S(1)} %get-tuple-element.946) | copy-start | bytes 1540
  13.2 28.2 %all-to-all-start.1 = ((s32[64,2,2]{1,2,0:T(2,128)}), s32[64,2,2]{1,2,0:T(2,128)S(1)}, u32[]{:S(2)}, u32[]{:S(2)}) async-start(s32[64,2,2]{1,2,0:T(2,128)} %copy.40), calls=%async_computation.1 | async-start | bytes 131072 | tf_op jit(solution)/shard_map/all_to_all | solution.py:125
  30.3 194.7 %all-gather.39.cloned.1.call-start = ((), (), s32[]{:S(2)}) async-start(), calls=%async_computation.10 | async-start | bytes 1179648 | tf_op jit(solution)/shard_map/all_gather | solution.py:11
  41.8 52.8 %copy-start.14 = (s32[128]{0:T(128)}, s32[128]{0:T(128)S(1)}, u32[]{:S(2)}) copy-start(s32[128]{0:T(128)S(1)} %min.56) | copy-start | bytes 1540
  44.3 49.5 %copy-start.16 = (pred[128]{0:T(512)(128)(4,1)}, pred[128]{0:T(512)(128)(4,1)S(1)}, u32[]{:S(2)}) copy-start(pred[128]{0:T(512)(128)(4,1)S(1)} %and_and_fusion.1) | copy-start | bytes 388
  46.3 48.3 %copy-start.19 = (s32[128]{0:T(128)S(1)}, s32[128]{0:T(128)}, u32[]{:S(2)}) copy-start(s32[128]{0:T(128)} %param.23) | copy-start | bytes 1540
  47.1 48.0 %all-to-all-start = ((bf16[64,2,1024]{2,1,0:T(2,128)(2,1)}), bf16[64,2,1024]{2,1,0:T(2,128)(2,1)S(1)}, u32[]{:S(2)}, u32[]{:S(2)}) async-start(bf16[64,2,1024]{2,1,0:T(2,128)(2,1)} %reshape.612), calls=%async_computation | async-start | bytes 524288 | tf_op jit(solution)/shard_map/all_to_all | solution.py:122
  51.8 174.2 %all-gather.37.cloned.1.call-start = ((), (), s32[]{:S(2)}) async-start(), calls=%async_computation.9 | async-start | bytes 1179648 | tf_op jit(solution)/shard_map/all_gather | solution.py:11
  51.8 43.7 %copy-start.1 = (bf16[1,256,384]{2,1,0:T(8,128)(2,1)S(1)}, bf16[1,256,384]{2,1,0:T(8,128)(2,1)}, u32[]{:S(2)}) copy-start(bf16[1,256,384]{2,1,0:T(8,128)(2,1)} %param.20) | copy-start | bytes 589828
  95.8 72.0 %copy-start.13 = (f32[128]{0:T(128)}, f32[128]{0:T(128)S(1)}, u32[]{:S(2)}) copy-start(f32[128]{0:T(128)S(1)} %get-tuple-element.951) | copy-start | bytes 1540
  96.8 158.0 %all-gather.35.cloned.1.call-start = ((), (), s32[]{:S(2)}) async-start(), calls=%async_computation.8 | async-start | bytes 4718592 | tf_op jit(solution)/shard_map/all_gather | solution.py:11
  124.2 131.7 %all-gather.33.cloned.1.call-start = ((), (), s32[]{:S(2)}) async-start(), calls=%async_computation.7 | async-start | bytes 4718592 | tf_op jit(solution)/shard_map/all_gather | solution.py:11
  128.8 23.6 %copy-start.7 = (bf16[1,1024,64]{1,2,0:T(8,128)(2,1)S(1)}, bf16[1,1024,64]{1,2,0:T(8,128)(2,1)}, u32[]{:S(2)}) copy-start(bf16[1,1024,64]{1,2,0:T(8,128)(2,1)} %param.19) | copy-start | bytes 393220
  129.9 198.9 %all-gather.31.cloned.1.call-start = ((), (), s32[]{:S(2)}) async-start(), calls=%async_computation.6 | async-start | bytes 2129920 | tf_op jit(solution)/shard_map/all_gather | solution.py:130
  132.2 20.8 %copy-start.11 = (pred[128]{0:T(512)(128)(4,1)}, pred[128]{0:T(512)(128)(4,1)S(1)}, u32[]{:S(2)}) copy-start(pred[128]{0:T(512)(128)(4,1)S(1)} %eq.89) | copy-start | bytes 388
  133.3 19.8 %copy-start.23 = (pred[128]{0:T(512)(128)(4,1)}, pred[128]{0:T(512)(128)(4,1)S(1)}, u32[]{:S(2)}) copy-start(pred[128]{0:T(512)(128)(4,1)S(1)} %and_and_fusion) | copy-start | bytes 388
  167.6 59.7 %copy-start.28 = (f32[1,1,128]{2,1,0:T(1,128)S(1)}, f32[1,1,128]{2,1,0:T(1,128)}, u32[]{:S(2)}) copy-start(f32[1,1,128]{2,1,0:T(1,128)} %get-tuple-element.921) | copy-start | bytes 1540
  257.0 26.2 %copy-start.12 = (pred[128]{0:T(512)(128)(4,1)S(1)}, pred[128]{0:T(512)(128)(4,1)}, u32[]{:S(2)}) copy-start(pred[128]{0:T(512)(128)(4,1)} %copy-done.11) | copy-start | bytes 388
  257.0 37.7 %copy-start.10 = (bf16[128,64]{0,1:T(8,128)(2,1)S(1)}, bf16[128,64]{0,1:T(8,128)(2,1)}, u32[]{:S(2)}) copy-start(bf16[128,64]{0,1:T(8,128)(2,1)} %copy-done.9) | copy-start | bytes 49156
  257.0 37.7 %copy-start.22 = (s32[128]{0:T(128)S(1)}, s32[128]{0:T(128)}, u32[]{:S(2)}) copy-start(s32[128]{0:T(128)} %copy-done.21) | copy-start | bytes 1540
  257.0 37.7 %copy-start.24 = (pred[128]{0:T(512)(128)(4,1)S(1)}, pred[128]{0:T(512)(128)(4,1)}, u32[]{:S(2)}) copy-start(pred[128]{0:T(512)(128)(4,1)} %copy-done.23) | copy-start | bytes 388
  257.0 38.8 %copy-start.6 = (bf16[128,256]{1,0:T(8,128)(2,1)S(1)}, bf16[128,256]{1,0:T(8,128)(2,1)}, u32[]{:S(2)}) copy-start(bf16[128,256]{1,0:T(8,128)(2,1)} %copy-done.5) | copy-start | bytes 196612
  257.0 38.8 %copy-start.15 = (s32[128]{0:T(128)S(1)}, s32[128]{0:T(128)}, u32[]{:S(2)}) copy-start(s32[128]{0:T(128)} %copy-done.14) | copy-start | bytes 1540
  257.0 38.8 %copy-start.17 = (pred[128]{0:T(512)(128)(4,1)S(1)}, pred[128]{0:T(512)(128)(4,1)}, u32[]{:S(2)}) copy-start(pred[128]{0:T(512)(128)(4,1)} %copy-done.16) | copy-start | bytes 388
  282.9 28.0 %copy-start.8 = (bf16[2,128,128]{2,1,0:T(8,128)(2,1)S(1)}, bf16[2,128,128]{2,1,0:T(8,128)(2,1)}, u32[]{:S(2)}) copy-start(bf16[2,128,128]{2,1,0:T(8,128)(2,1)} %param.14) | copy-start | bytes 196612
  284.8 20.7 %all-to-all-start.3 = ((bf16[64,2,128]{2,1,0:T(2,128)(2,1)}), bf16[64,2,128]{2,1,0:T(2,128)(2,1)S(1)}, u32[]{:S(2)}, u32[]{:S(2)}) async-start(bf16[64,2,128]{2,1,0:T(2,128)(2,1)} %bitcast.71), calls=%async_computation.3 | async-start | bytes 65536 | tf_op jit(solution)/shard_map/all_to_all | solution.py:213
  305.5 28.3 %all-to-all-start.2 = ((bf16[64,1,2]{2,1,0:T(2,128)(2,1)}), bf16[64,1,2]{2,1,0:T(2,128)(2,1)S(1)}, u32[]{:S(2)}, u32[]{:S(2)}) async-start(bf16[64,1,2]{2,1,0:T(2,128)(2,1)} %convert_element_type.153), calls=%async_computation.2 | async-start | bytes 65536 | tf_op jit(solution)/shard_map/all_to_all | solution.py:220
  310.1 56.8 %reduce-scatter.4.cloned.1.call-start = ((), (), s32[]{:S(2)}) async-start(), calls=%async_computation.11 | async-start | bytes 294912
  (8 other events, 40.8 us)
Sparse Core Ops, SparseCore 0:
  11.0 94.3 all-gather.28
  108.2 28.4 all-gather.38
  139.4 28.8 all-gather.36
  170.3 37.4 all-gather.34
  209.8 37.3 all-gather.32
  250.0 78.7 all-gather.30
  332.2 34.6 reduce-scatter.3
where the time goes:
time: 377 us; the launch traced here: 375 us
  blocking collectives  154 us (41%)
  waiting for transfers between devices  74.4 us (20%)
  local copies, waits for them, and re-layouts  39.3 us (10%)
  starting transfers between devices  36.7 us (10%)
  other arithmetic  35.9 us (10%)
  matrix products  19.2 us (5%)
  between operations  15 us (4%)
    all_gather x11, blocking collectives, merged(): everything = jax.tree.map(lambda part: lax.all_gather(part, axis), x)  113 us
    all_gather x1, blocking collectives, on_device(): lax.all_gather(cluster_weight, 'tok', axis=0, tiled=True)  41.8 us
    unnamed x8, waiting for transfers between devices  32.2 us
    add x21, other arithmetic, joined(): left_side[3] + right_side[3]  24.6 us
    all_gather x1, waiting for transfers between devices, on_device(): lax.all_gather(conv_weight, 'tok', axis=2, tiled=True)  17.7 us
    all_to_all x1, starting transfers between devices, on_device(): lax.all_to_all(send_meta.reshape(owners, capacity, 2), 'tok', split_axis=...  17.1 us
    all_to_all x1, waiting for transfers between devices, on_device(): lax.all_to_all(send_meta.reshape(owners, capacity, 2), 'tok', split_axis=...  9.96 us
    all_to_all x1, starting transfers between devices, on_device(): lax.all_to_all(tail_back.reshape(owners, capacity, narrow).astype(jnp.bfl...  9.89 us
  transfers between devices with their start and end apart: 11, of which 5 were waited for; matrix products, arithmetic and copies ran while one was open for 24% of the time, Pallas kernels for 0%

commit v1 on v0

v1 whole, which is shorter than its diff:
```python
import functools

import jax
import jax.numpy as jnp
from jax import lax
from jax.experimental import pallas as pl
from jax.experimental.pallas import tpu as pltpu
from jax.sharding import PartitionSpec as P

K = 4
LEN = 128
T = 128
D = 1024
OWN = 64
NCH = 8
NAR = 128
HW = 2560
CW = 16
GW = HW + CW
HP = 2688
BLK = 384
CONV = 2 * K * NAR
W1 = 384
W2 = 1152
P1 = 256
P2 = 64
SROW = 16
NEG = -1e30
f32 = jnp.float32
bf16 = jnp.bfloat16
VMEM = pl.BlockSpec(memory_space=pltpu.VMEM)
SMEM = pl.BlockSpec(memory_space=pltpu.SMEM)
ANY = pl.BlockSpec(memory_space=pl.ANY)


def dot(a, b, ca=1, cb=0):
    return lax.dot_general(a, b, (((ca,), (cb,)), ((), ())), preferred_element_type=f32)


def parts3(x):
    hi = x.astype(bf16).astype(f32)
    rest = x - hi
    mid = rest.astype(bf16).astype(f32)
    return [hi, mid, rest - mid]


def iota(shape, axis):
    return lax.broadcasted_iota(jnp.int32, shape, axis)


def call(kernel, outs, *args, specs=None, scratch=(), flops=10**7, nbytes=10**6):
    outs = [jax.ShapeDtypeStruct(shape, kind) for shape, kind in outs]
    return pl.pallas_call(
        kernel,
        out_shape=outs,
        in_specs=[VMEM] * len(args) if specs is None else specs,
        out_specs=[VMEM] * len(outs),
        scratch_shapes=list(scratch),
        cost_estimate=pl.CostEstimate(flops=flops, bytes_accessed=nbytes, transcendentals=0),
    )(*args)


def route_kernel(cid_row, cid_col, tgt_col, hidden, send, pick):
    owner_row = jnp.where(cid_row[...] >= 0, cid_row[...] // 2, -1)
    owner_col = jnp.where(cid_col[...] >= 0, cid_col[...] // 2, -2)
    before = (owner_col == owner_row) & (iota((T, T), 0) < iota((T, T), 1))
    rank = jnp.sum(before.astype(f32), axis=0, keepdims=True).astype(jnp.int32)
    slot = jnp.where(owner_row >= 0, owner_row * 2 + rank, -1)
    chosen = (iota((T, T), 0) == slot).astype(bf16)
    pick[...] = chosen
    send[:, :D] = dot(chosen, hidden[...]).astype(bf16)
    lane = iota((T, 128), 1)
    word = tgt_col[...]
    tier = jnp.where(cid_col[...] >= 0, cid_col[...] % 2 + 1, 0)
    meta = jnp.where(lane == 0, word // 128, jnp.where(lane == 1, word % 128, jnp.where(lane == 2, tier, 0)))
    send[:, D:] = dot(chosen, meta.astype(f32).astype(bf16)).astype(bf16)


def slot_meta(meta):
    meta = meta.astype(f32)
    word = (meta[:, 0:1] * 128.0 + meta[:, 1:2]).astype(jnp.int32)
    tier = meta[:, 2:3].astype(jnp.int32)
    return word, tier


def tail_kernel(ch, rows, meta, proj1, proj2, out1, out2, feat, part):
    word, tier = slot_meta(meta[...])
    first = tier == 1
    z1 = dot(rows[...], proj1[...])
    z2 = dot(rows[...], proj2[...])
    features = jnp.where(first, z1, z2).astype(bf16)
    feat[...] = features

    def local(out, width):
        logits = dot(features, out[...])
        top = jnp.max(logits, axis=1, keepdims=True)
        terms = jnp.exp(logits - top)
        total = jnp.sum(terms, axis=1, keepdims=True)
        hot = iota((T, width), 1) == word - ch[0] * width
        target = jnp.sum(jnp.where(hot, logits, 0.0), axis=1, keepdims=True)
        value = dot(jnp.where(hot, 0.0, terms).astype(bf16), out[...], 1, 1)
        column = dot(hot.astype(f32).astype(bf16), out[...], 1, 1)
        return top, total, target, value, column

    one = local(out1, W1)
    two = local(out2, W2)
    top, total, target, value, column = [jnp.where(first, a, b) for a, b in zip(one, two)]
    part[:, :P1] = value.astype(bf16)
    part[:, P1 : 2 * P1] = column.astype(bf16)
    lane = iota((T, 128), 1)
    stats = jnp.zeros((T, 128), f32)
    for i, x in enumerate(parts3(top) + parts3(total) + parts3(target)):
        stats = jnp.where(lane == i, x, stats)
    part[:, 2 * P1 :] = stats.astype(bf16)


def tail_merge_kernel(meta, parts, proj1_part, proj2_part, dz1, dz2, log_total, back):
    _, tier = slot_meta(meta[...])
    tops, totals, target = [], [], 0.0
    for g in range(NCH):
        stats = parts[g, :, 2 * P1 :].astype(f32)
        s3 = [stats[:, i : i + 1] for i in range(9)]
        tops.append(s3[0] + s3[1] + s3[2])
        totals.append(s3[3] + s3[4] + s3[5])
        target = target + (s3[6] + s3[7] + s3[8])
    top = functools.reduce(jnp.maximum, tops)
    scales = [jnp.exp(t - top) for t in tops]
    total = sum(s * t for s, t in zip(scales, totals))
    log_all = top + jnp.log(total)
    inverse = 1.0 / total
    value = jnp.zeros((T, P1), f32)
    column = jnp.zeros((T, P1), f32)
    for g in range(NCH):
        value = value + parts[g, :, :P1].astype(f32) * (scales[g] * inverse)
        column = column + parts[g, :, P1 : 2 * P1].astype(f32)
    dz = value + (jnp.exp(target - log_all) - 1.0) * column
    one = jnp.where(tier == 1, dz, 0.0).astype(bf16)
    two = jnp.where(tier == 2, dz, 0.0).astype(bf16)
    dz1[...] = one
    dz2[...] = two
    log_total[...] = jnp.broadcast_to(log_all, (T, 128))
    back[:, :NAR] = (dot(one, proj1_part[...], 1, 1) + dot(two, proj2_part[...], 1, 1)).astype(bf16)
    loss = jnp.where(tier > 0, log_all - target, 0.0)
    lane = iota((T, 128), 1)
    tail = jnp.zeros((T, 128), f32)
    for i, x in enumerate(parts3(loss)):
        tail = jnp.where(lane == i, x, tail)
    back[:, NAR:] = tail.astype(bf16)


def tail_grad_kernel(ch, meta, feat, rows_part, dz1, dz2, log_total, out1, out2, g_out1, g_out2, g_proj1, g_proj2):
    word, tier = slot_meta(meta[...])
    features = feat[...]
    log_all = log_total[:, 0:1]

    def slope(out, width, which):
        logits = dot(features, out[...])
        hot = (iota((T, width), 1) == word - ch[0] * width).astype(f32)
        return jnp.where(tier == which, jnp.exp(logits - log_all) - hot, 0.0).astype(bf16)

    g_out1[...] = dot(features, slope(out1, W1, 1), 0, 0)
    g_out2[...] = dot(features, slope(out2, W2, 2), 0, 0)[:P2]
    g_proj1[...] = dot(rows_part[...], dz1[...], 0, 0)
    g_proj2[...] = dot(rows_part[...], dz2[...], 0, 0)[:, :P2]


def back_kernel(got, pick, back_t, loss):
    back_t[...] = dot(got[:, :NAR], pick[...], 0, 0)
    terms = dot(got[:, NAR:], pick[...], 0, 0)
    loss[...] = terms[0:1] + terms[1:2] + terms[2:3]


def head_kernel(col, hidden, weight, out, acc, stat):
    step = pl.program_id(0)

    @pl.when(step == 0)
    def _():
        acc[...] = jnp.zeros_like(acc)
        stat[0:1, :] = jnp.full((1, T), NEG, f32)
        stat[1:2, :] = jnp.zeros((1, T), f32)
        stat[2:3, :] = jnp.zeros((1, T), f32)

    logits = dot(hidden[...], weight[...]).T
    index = iota((BLK, T), 0) + step * BLK
    logits = jnp.where(index < GW, logits, NEG)
    old = stat[0:1, :]
    top = jnp.maximum(old, jnp.max(logits, axis=0, keepdims=True))
    scale = jnp.exp(old - top)
    terms = jnp.exp(logits - top)
    hot = index == col[...]
    stat[0:1, :] = top
    stat[1:2, :] = stat[1:2, :] * scale + jnp.sum(terms, axis=0, keepdims=True)
    stat[2:3, :] = stat[2:3, :] + jnp.sum(jnp.where(hot, logits, 0.0), axis=0, keepdims=True)
    right = jnp.concatenate([jnp.where(hot, 0.0, terms), hot.astype(f32)], axis=1).astype(bf16)
    new = dot(weight[...], right)
    acc[:, :T] = acc[:, :T] * scale + new[:, :T]
    acc[:, T:] = acc[:, T:] + new[:, T:]

    @pl.when(step == pl.num_programs(0) - 1)
    def _():
        line = iota((SROW, 2 * T), 0)
        stats = jnp.zeros((SROW, 2 * T), f32)
        rows = parts3(stat[0:1, :]) + parts3(stat[1:2, :]) + parts3(stat[2:3, :])
        for i, x in enumerate(rows):
            stats = jnp.where(line == i, jnp.concatenate([x, x], axis=1), stats)
        for g in range(NCH):
            out[g, :NAR, :] = acc[g * NAR : (g + 1) * NAR, :].astype(bf16)
            out[g, NAR:, :] = stats.astype(bf16)


def head_call(col, hidden, weight):
    return pl.pallas_call(
        head_kernel,
        out_shape=jax.ShapeDtypeStruct((NCH, NAR + SROW, 2 * T), bf16),
        grid=(HP // BLK,),
        in_specs=[
            pl.BlockSpec((1, T), lambda i: (0, 0)),
            pl.BlockSpec((T, D), lambda i: (0, 0)),
            pl.BlockSpec((D, BLK), lambda i: (0, i)),
        ],
        out_specs=pl.BlockSpec((NCH, NAR + SROW, 2 * T), lambda i: (0, 0, 0)),
        scratch_shapes=[pltpu.VMEM((D, 2 * T), f32), pltpu.VMEM((8, T), f32)],
        compiler_params=pltpu.CompilerParams(dimension_semantics=("arbitrary",)),
        cost_estimate=pl.CostEstimate(flops=2 * 10**9, bytes_accessed=6 * 10**6, transcendentals=0),
    )(col, hidden, weight)


def conv_kernel(parts, back_t, tail_loss, gates, weight, conv, grad, loss, taps, wide, sem):
    copy = pltpu.make_async_copy(weight.at[:, pl.ds(HP, CONV)], wide, sem)
    copy.start()
    tops, totals, target = [], [], 0.0
    for g in range(NCH):
        stats = parts[g, NAR:, :T].astype(f32)
        s3 = [stats[i : i + 1] for i in range(9)]
        tops.append(s3[0] + s3[1] + s3[2])
        totals.append(s3[3] + s3[4] + s3[5])
        target = target + (s3[6] + s3[7] + s3[8])
    top = functools.reduce(jnp.maximum, tops)
    scales = [jnp.exp(t - top) for t in tops]
    total = sum(s * t for s, t in zip(scales, totals))
    log_all = top + jnp.log(total)
    inverse = 1.0 / total
    loss[...] = log_all - target + tail_loss[...]
    dh = back_t[...]
    column = jnp.zeros((NAR, T), f32)
    for g in range(NCH):
        dh = dh + parts[g, :NAR, :T].astype(f32) * (scales[g] * inverse)
        column = column + parts[g, :NAR, T:].astype(f32)
    dh = dh + (jnp.exp(target - log_all) - 1.0) * column
    grad[...] = dh
    a = gates[0].astype(f32)
    sig = 1.0 / (1.0 + jnp.exp(-gates[1].astype(f32)))
    da = dh * sig
    db = da * a * (1.0 - sig)
    lane = iota((NAR, T), 1)
    for half, value in enumerate((da, db)):
        for k in range(K):
            moved = value if k == 0 else jnp.where(lane < T - k, pltpu.roll(value, T - k, 1), 0.0)
            at = (half * K + k) * NAR
            taps[at : at + NAR, :] = moved.astype(bf16)
    copy.wait()
    total_conv = dot(wide[...], taps[...])
    for g in range(NCH):
        conv[g] = total_conv[g * NAR : (g + 1) * NAR].astype(bf16)


def final_kernel(parts, grad, out):
    total = grad[...]
    for g in range(NCH):
        total = total + parts[g].astype(f32)
    out[...] = total.T.astype(bf16)


def on_device(hidden, pre_gates, conv_weight, head_weight, cluster_weight, tail1_proj, tail2_proj, tail1_out, tail2_out, cluster_id, target):
    ch = lax.axis_index("ch").astype(jnp.int32)
    ch_arr = ch.reshape(1)
    packed = jnp.concatenate(
        [
            head_weight,
            cluster_weight,
            jnp.zeros((head_weight.shape[0], HP - GW), bf16),
            conv_weight.transpose(2, 0, 1, 3).reshape(head_weight.shape[0], CONV),
        ],
        axis=1,
    )
    gathered = lax.all_gather(packed, "tok", axis=0, tiled=True)

    send, pick = call(
        route_kernel,
        [((T, D + 128), bf16), ((T, T), bf16)],
        cluster_id.reshape(1, T),
        cluster_id.reshape(T, 1),
        target.reshape(T, 1),
        hidden,
    )
    got = lax.all_to_all(send.reshape(OWN, 2, D + 128), "tok", split_axis=0, concat_axis=0, tiled=True).reshape(T, D + 128)
    rows, meta = got[:, :D], got[:, D:]
    proj1 = tail1_proj[0]
    proj2 = jnp.pad(tail2_proj[0], ((0, 0), (0, P1 - P2)))
    out1 = tail1_out[0]
    out2 = jnp.pad(tail2_out[0], ((0, P1 - P2), (0, 0)))
    col_start = ch * NAR
    proj1_part = lax.dynamic_slice_in_dim(proj1, col_start, NAR, 0)
    proj2_part = lax.dynamic_slice_in_dim(proj2, col_start, NAR, 0)
    rows_part = lax.dynamic_slice_in_dim(rows, col_start, NAR, 1)
    feat, part = call(
        tail_kernel,
        [((T, P1), bf16), ((T, 2 * P1 + 128), bf16)],
        ch_arr, rows, meta, proj1, proj2, out1, out2,
        specs=[SMEM] + [VMEM] * 6,
    )
    parts = lax.all_to_all(
        jnp.broadcast_to(part[None], (NCH,) + part.shape), "ch", split_axis=0, concat_axis=0, tiled=True
    )
    dz1, dz2, log_total, back = call(
        tail_merge_kernel,
        [((T, P1), bf16), ((T, P1), bf16), ((T, 128), f32), ((T, NAR + 128), bf16)],
        meta, parts, proj1_part, proj2_part,
    )
    got_back = lax.all_to_all(back.reshape(OWN, 2, NAR + 128), "tok", split_axis=0, concat_axis=0, tiled=True).reshape(T, NAR + 128)
    g_out1, g_out2, g_proj1, g_proj2 = call(
        tail_grad_kernel,
        [((P1, W1), f32), ((P2, W2), f32), ((NAR, P1), f32), ((NAR, P2), f32)],
        ch_arr, meta, feat, rows_part, dz1, dz2, log_total, out1, out2,
        specs=[SMEM] + [VMEM] * 8,
    )
    back_t, tail_loss = call(back_kernel, [((NAR, T), f32), ((1, T), f32)], got_back, pick)

    is_tail = cluster_id >= 0
    word_local = target - ch * HW
    cluster_local = cluster_id - ch * CW
    local = jnp.where(
        is_tail,
        jnp.where((cluster_local >= 0) & (cluster_local < CW), HW + cluster_local, -1),
        jnp.where((word_local >= 0) & (word_local < HW), word_local, -1),
    )
    gathered, back_t = lax.optimization_barrier((gathered, back_t))
    head = head_call(local.reshape(1, T), hidden, gathered)
    head_parts = lax.all_to_all(head, "ch", split_axis=0, concat_axis=0, tiled=True)
    conv, grad, loss = call(
        conv_kernel,
        [((NCH, NAR, T), bf16), ((NAR, T), f32), ((1, T), f32)],
        head_parts, back_t, tail_loss, pre_gates.transpose(0, 2, 1), gathered,
        specs=[VMEM] * 4 + [ANY],
        scratch=[pltpu.VMEM((CONV, T), bf16), pltpu.VMEM((D, CONV), bf16), pltpu.SemaphoreType.DMA],
    )
    conv_parts = lax.all_to_all(conv, "ch", split_axis=0, concat_axis=0, tiled=True)
    (grad_input,) = call(final_kernel, [((T, NAR), bf16)], conv_parts, grad)
    return (loss.reshape(T), grad_input, g_proj1[None], g_proj2[None], g_out1[None], g_out2[None])


def solution(mesh):
    placed = (
        P("tok", None),
        P(None, "tok", "ch"),
        P(None, None, "tok", "ch"),
        P("tok", "ch"),
        P("tok", "ch"),
        P("tok", None, None),
        P("tok", None, None),
        P("tok", None, "ch"),
        P("tok", None, "ch"),
        P("tok"),
        P("tok"),
    )
    return jax.shard_map(
        on_device,
        mesh=mesh,
        in_specs=placed,
        out_specs=(
            P("tok"),
            P("tok", "ch"),
            P("tok", "ch", None),
            P("tok", "ch", None),
            P("tok", None, "ch"),
            P("tok", None, "ch"),
        ),
        check_vma=False,
    )
```

time: 377 us -> 167 us (0.44)
  blocking collectives: 154 us -> 0 us
  other arithmetic: 35.9 us -> 0.52 us
  Pallas kernels: 0 us -> 28.3 us
  matrix products: 19.2 us -> 0 us
  local copies, waits for them, and re-layouts: 39.3 us -> 23.2 us
  waiting for transfers between devices: 74.4 us -> 62.1 us
    all_gather x12 -> x0, blocking collectives: 154 us -> none  [the longest x11 113 us: merged(): everything = jax.tree.map(lambda part: lax.all_gather(part, axis), x)]
    all_to_all x4 -> x5, waiting for transfers between devices: 17.7 us -> 50.2 us  [the longest x1 15.7 us: on_device(): lax.all_to_all(jnp.broadcast_to(part[None], (NCH,) + part.shape), 'ch', s...]
    unnamed x8 -> x1, waiting for transfers between devices: 32.2 us -> 0.02 us
    pallas_call x0 -> x8, Pallas kernels: none -> 28.3 us  [the longest x7 19.1 us: call(): pl.pallas_call(kernel, out_shape=outs, in_specs=[VMEM] * len(args) if spe...]
    add x58 -> x0, other arithmetic: 27.1 us -> none  [the longest x21 24.6 us: joined(): left_side[3] + right_side[3]]
    dot_general x17 -> x0, matrix products: 19.2 us -> none  [the longest x1 4.36 us: on_device(): jnp.dot(word_terms.astype(jnp.bfloat16), head_full.T, preferred_element_t...]
    gather x10 -> x0, local copies, waits for them, and re-layouts: 14.5 us -> none  [the longest x1 4.23 us: on_device(): word_vector = jnp.take(head_full, word_column, axis=1).T.astype(jnp.float32)]
    all_gather x6 -> x1, waiting for transfers between devices: 24.5 us -> 11.9 us  [on_device(): gathered = lax.all_gather(packed, 'tok', axis=0, tiled=True)]
  transfers between devices with their start and end apart: 11 -> 6, of which waited for: 5 -> 6; matrix products, arithmetic and copies ran while one was open for 24% -> 11% of each run, Pallas kernels for 0% -> 8%
where the time goes in v1:
time: 167 us; the launch traced here: 166 us
  waiting for transfers between devices  62.1 us (37%)
  starting transfers between devices  37.9 us (23%)
  Pallas kernels  28.3 us (17%)
  local copies, waits for them, and re-layouts  23.2 us (14%)
  between operations  14.1 us (8%)
    pallas_call x7, Pallas kernels, call(): pl.pallas_call(kernel, out_shape=outs, in_specs=[VMEM] * len(args) if spe...  19.1 us
    all_to_all x1, starting transfers between devices, on_device(): lax.all_to_all(send.reshape(OWN, 2, D + 128), 'tok', split_axis=0, concat...  17.1 us
    all_to_all x1, waiting for transfers between devices, on_device(): lax.all_to_all(jnp.broadcast_to(part[None], (NCH,) + part.shape), 'ch', s...  15.7 us
    all_to_all x1, waiting for transfers between devices, on_device(): lax.all_to_all(send.reshape(OWN, 2, D + 128), 'tok', split_axis=0, concat...  13.2 us
    all_gather x1, waiting for transfers between devices, on_device(): gathered = lax.all_gather(packed, 'tok', axis=0, tiled=True)  11.9 us
    all_to_all x1, waiting for transfers between devices, on_device(): lax.all_to_all(back.reshape(OWN, 2, NAR + 128), 'tok', split_axis=0, conc...  11.2 us
    all_to_all x1, waiting for transfers between devices, on_device(): lax.all_to_all(head, 'ch', split_axis=0, concat_axis=0, tiled=True)  9.31 us
    pallas_call x1, Pallas kernels, head_call(): pl.pallas_call(head_kernel, out_shape=jax.ShapeDtypeStruct((NCH, NAR + SR...  9.2 us
  transfers between devices with their start and end apart: 6, of which 6 were waited for; matrix products, arithmetic and copies ran while one was open for 11% of the time, Pallas kernels for 8%

profile of v1, /device:TPU:1, one launch (start us, length us, event | category | flops | bytes accessed | tf_op | source)
XLA Modules:
  0.0 166.1 jit_solution(5959977534161691728)
XLA Ops:
  7.2 0.8 copy.17
  8.1 1.6 concatenate.3
  9.7 1.4 copy.18.cid_col
  11.1 1.4 copy.19.tgt_col
  12.5 2.1 %shard_map.154 = (bf16[128,1152]{1,0:T(8,128)(2,1)}, bf16[128,128]{1,0:T(8,128)(2,1)}) custom-call(s32[1,128]{1,0:T(1,128)} %bitcast.29, s32[128,1]{1,0:T(8,128)} %copy.18.cid_col, s32[128,1]{1,0:T(8,128)} %copy.19.tgt_col, bf16[128,1024]{1,0:T(8,128)(2,1)} %hidden.3), custom_call_target="tpu_custom_call" | custom-call | flops 10000000 | bytes 1000000 | tf_op jit(solution)/shard_map/pallas_call | solution.py:53
  14.6 1.8 %reshape.52 = bf16[64,2,1152]{2,1,0:T(2,128)(2,1)} reshape(bf16[128,1152]{1,0:T(8,128)(2,1)} %get-tuple-element.25) | data formatting | bytes 589824 | tf_op jit(solution)/shard_map/reshape | solution.py:296
  16.4 17.1 %all-to-all-start = ((bf16[64,2,1152]{2,1,0:T(2,128)(2,1)}), bf16[64,2,1152]{2,1,0:T(2,128)(2,1)S(1)}, u32[]{:S(2)}, u32[]{:S(2)}) async-start(bf16[64,2,1152]{2,1,0:T(2,128)(2,1)} %reshape.52), calls=%async_computation | async-start | bytes 589824 | tf_op jit(solution)/shard_map/all_to_all | solution.py:296
  33.7 0.9 pad.8.proj2
  34.7 0.9 pad.9.out2
  35.5 13.2 %all-to-all-done = bf16[64,2,1152]{2,1,0:T(2,128)(2,1)S(1)} async-done(((bf16[64,2,1152]{2,1,0:T(2,128)(2,1)}), bf16[64,2,1152]{2,1,0:T(2,128)(2,1)S(1)}, u32[]{:S(2)}, u32[]{:S(2)}) %all-to-all-start) | async-done | bytes 294944 | tf_op jit(solution)/shard_map/all_to_all | solution.py:296
  50.2 3.7 %shard_map.155 = (bf16[128,256]{1,0:T(8,128)(2,1)}, bf16[128,640]{1,0:T(8,128)(2,1)}) custom-call(s32[1]{0:T(128)} %bitcast.5.ch, bf16[128,1024]{1,0:T(8,128)(2,1)} %slice.9.rows, bf16[128,128]{1,0:T(8,128)(2,1)} %slice.8.meta, bf16[1024,256]{1,0:T(8,128)(2,1)} %bitcast.23, bf16[1024,256]{1,0:T(8,128)(2,1)} %pad.8.proj2, bf16[256,384]{1,0:T(8,128)(2,1)} %bitcast.21, ...), custom_call_target="tpu_custom_call" | custom-call | flops 10000000 | bytes 1000000 | tf_op jit(solution)/shard_map/pallas_call | solution.py:53
  53.9 2.1 %broadcast_in_dim.28 = bf16[8,128,640]{2,1,0:T(8,128)(2,1)} broadcast(bf16[128,640]{1,0:T(8,128)(2,1)} %get-tuple-element.26), dimensions={1,2} | broadcast | bytes 1474560 | tf_op jit(solution)/shard_map/broadcast_in_dim | solution.py:313
  56.1 6.4 %all-to-all-start.1 = ((bf16[8,128,640]{2,1,0:T(8,128)(2,1)}), bf16[8,128,640]{2,1,0:T(8,128)(2,1)S(1)}, u32[]{:S(2)}, u32[]{:S(2)}) async-start(bf16[8,128,640]{2,1,0:T(8,128)(2,1)} %broadcast_in_dim.28), calls=%async_computation.1 | async-start | bytes 2621440 | tf_op jit(solution)/shard_map/all_to_all | solution.py:312
  63.2 1.5 dynamic-slice_bitcast_fusion.proj1_part
  64.6 15.7 %all-to-all-done.1.parts = bf16[8,128,640]{2,1,0:T(8,128)(2,1)S(1)} async-done(((bf16[8,128,640]{2,1,0:T(8,128)(2,1)}), bf16[8,128,640]{2,1,0:T(8,128)(2,1)S(1)}, u32[]{:S(2)}, u32[]{:S(2)}) %all-to-all-start.1) | async-done | bytes 1310752 | tf_op jit(solution)/shard_map/all_to_all | solution.py:312
  80.3 1.1 copy-done
  81.4 2.9 %shard_map.156 = (bf16[128,256]{1,0:T(8,128)(2,1)}, bf16[128,256]{1,0:T(8,128)(2,1)}, f32[128,128]{1,0:T(8,128)}, bf16[128,256]{1,0:T(8,128)(2,1)}) custom-call(bf16[128,128]{1,0:T(8,128)(2,1)} %slice.8.meta, bf16[8,128,640]{2,1,0:T(8,128)(2,1)} %copy-done, bf16[128,256]{1,0:T(8,128)(2,1)} %dynamic-slice_bitcast_fusion.proj1_part, ...), custom_call_target="tpu_custom_call" | custom-call | flops 10000000 | bytes 1000000 | tf_op jit(solution)/shard_map/pallas_call | solution.py:53
  84.3 1.5 reshape.55
  85.8 4.6 %all-to-all-start.2 = ((bf16[64,2,256]{2,1,0:T(2,128)(2,1)}), bf16[64,2,256]{2,1,0:T(2,128)(2,1)S(1)}, u32[]{:S(2)}, u32[]{:S(2)}) async-start(bf16[64,2,256]{2,1,0:T(2,128)(2,1)} %reshape.55), calls=%async_computation.2 | async-start | bytes 131072 | tf_op jit(solution)/shard_map/all_to_all | solution.py:320
  91.0 11.2 %all-to-all-done.2 = bf16[64,2,256]{2,1,0:T(2,128)(2,1)S(1)} async-done(((bf16[64,2,256]{2,1,0:T(2,128)(2,1)}), bf16[64,2,256]{2,1,0:T(2,128)(2,1)S(1)}, u32[]{:S(2)}, u32[]{:S(2)}) %all-to-all-start.2) | async-done | bytes 65568 | tf_op jit(solution)/shard_map/all_to_all | solution.py:320
  102.9 1.7 %shard_map.157 = (f32[128,128]{1,0:T(8,128)}, f32[1,128]{1,0:T(1,128)}) custom-call(bf16[128,256]{1,0:T(8,128)(2,1)} %reshape.56.got, bf16[128,128]{1,0:T(8,128)(2,1)} %get-tuple-element.28.pick), custom_call_target="tpu_custom_call" | custom-call | flops 10000000 | bytes 1000000 | tf_op jit(solution)/shard_map/pallas_call | solution.py:53
  104.6 11.9 %all-gather.2.cloned.1.call-done.weight = bf16[1024,3712]{1,0:T(8,128)(2,1)} async-done(((bf16[16,3712]{1,0:T(8,128)(2,1)}), bf16[1024,3712]{1,0:T(8,128)(2,1)}) %all-gather.2.cloned.1.call-update) | async-done | bytes 7602192 | tf_op jit(solution)/shard_map/all_gather | solution.py:286
  116.5 9.2 %shard_map.158 = bf16[8,144,256]{2,1,0:T(8,128)(2,1)} custom-call(s32[1,128]{1,0:T(1,128)} %fusion.col, bf16[128,1024]{1,0:T(8,128)(2,1)} %hidden.3, bf16[1024,3712]{1,0:T(8,128)(2,1)} %all-gather.2.cloned.1.call-done.weight), custom_call_target="tpu_custom_call" | custom-call | flops 2000000000 | bytes 6000000 | tf_op jit(solution)/shard_map/pallas_call | solution.py:212
  125.7 5.4 %all-to-all-start.3 = ((bf16[8,144,256]{2,1,0:T(8,128)(2,1)}), bf16[8,144,256]{2,1,0:T(8,128)(2,1)S(1)}, u32[]{:S(2)}, u32[]{:S(2)}) async-start(bf16[8,144,256]{2,1,0:T(8,128)(2,1)} %shard_map.158), calls=%async_computation.3 | async-start | bytes 1179648 | tf_op jit(solution)/shard_map/all_to_all | solution.py:339
  131.8 9.3 %all-to-all-done.3.parts = bf16[8,144,256]{2,1,0:T(8,128)(2,1)S(1)} async-done(((bf16[8,144,256]{2,1,0:T(8,128)(2,1)}), bf16[8,144,256]{2,1,0:T(8,128)(2,1)S(1)}, u32[]{:S(2)}, u32[]{:S(2)}) %all-to-all-start.3) | async-done | bytes 589856 | tf_op jit(solution)/shard_map/all_to_all | solution.py:339
  141.1 0.9 copy-done.1
  142.0 4.1 %shard_map.159 = (bf16[8,128,128]{2,1,0:T(8,128)(2,1)}, f32[128,128]{1,0:T(8,128)}, f32[1,128]{1,0:T(1,128)}) custom-call(bf16[8,144,256]{2,1,0:T(8,128)(2,1)} %copy-done.1, f32[128,128]{1,0:T(8,128)} %get-tuple-element.31.back_t, f32[1,128]{1,0:T(1,128)} %get-tuple-element.32.tail_loss, bf16[2,128,128]{2,1,0:T(8,128)(2,1)} %bitcast.24, ...), custom_call_target="tpu_custom_call" | custom-call | flops 10000000 | bytes 1000000 | tf_op jit(solution)/shard_map/pallas_call | solution.py:53
  146.1 4.3 %all-to-all-start.4 = ((bf16[8,128,128]{2,1,0:T(8,128)(2,1)}), bf16[8,128,128]{2,1,0:T(8,128)(2,1)S(1)}, u32[]{:S(2)}, u32[]{:S(2)}) async-start(bf16[8,128,128]{2,1,0:T(8,128)(2,1)} %get-tuple-element.34), calls=%async_computation.4 | async-start | bytes 524288 | tf_op jit(solution)/shard_map/all_to_all | solution.py:347
  150.4 1.4 constant_dynamic-slice_fusion.rows_part
  151.8 2.8 %shard_map.161 = (f32[256,384]{1,0:T(8,128)}, f32[64,1152]{1,0:T(8,128)}, f32[128,256]{1,0:T(8,128)}, f32[128,64]{1,0:T(8,128)}) custom-call(s32[1]{0:T(128)} %bitcast.5.ch, bf16[128,128]{1,0:T(8,128)(2,1)} %slice.8.meta, bf16[128,256]{1,0:T(8,128)(2,1)} %get-tuple-element.36.feat, bf16[128,128]{1,0:T(8,128)(2,1)} %constant_dynamic-slice_fusion.rows_part, ...), custom_call_target="tpu_custom_call" | custom-call | flops 10000000 | bytes 1000000 | tf_op jit(solution)/shard_map/pallas_call | solution.py:53
  154.6 1.5 copy.22
  157.6 1.7 %shard_map.160 = bf16[128,128]{1,0:T(8,128)(2,1)} custom-call(bf16[8,128,128]{2,1,0:T(8,128)(2,1)} %copy-done.2, f32[128,128]{1,0:T(8,128)} %get-tuple-element.35.grad), custom_call_target="tpu_custom_call" | custom-call | flops 10000000 | bytes 1000000 | tf_op jit(solution)/shard_map/pallas_call | solution.py:53
  (27 shorter events, 5.8 us)
Async XLA Ops:
  7.2 26.4 %copy-start.4 = (bf16[1,1024,64]{1,2,0:T(8,128)(2,1)S(1)}, bf16[1,1024,64]{1,2,0:T(8,128)(2,1)}, u32[]{:S(2)}) copy-start(bf16[1,1024,64]{1,2,0:T(8,128)(2,1)} %param.17) | copy-start | bytes 393220
  7.2 109.3 %all-gather.2.cloned.1.call-start = ((), (), s32[]{:S(2)}) async-start(), calls=%async_computation.5 | async-start | bytes 7720960 | tf_op jit(solution)/shard_map/all_gather | solution.py:286
  12.5 22.2 %copy-start.3 = (bf16[1,64,1152]{2,1,0:T(8,128)(2,1)S(1)}, bf16[1,64,1152]{2,1,0:T(8,128)(2,1)}, u32[]{:S(2)}) copy-start(bf16[1,64,1152]{2,1,0:T(8,128)(2,1)} %param.19) | copy-start | bytes 442372
  16.4 32.3 %all-to-all-start = ((bf16[64,2,1152]{2,1,0:T(2,128)(2,1)}), bf16[64,2,1152]{2,1,0:T(2,128)(2,1)S(1)}, u32[]{:S(2)}, u32[]{:S(2)}) async-start(bf16[64,2,1152]{2,1,0:T(2,128)(2,1)} %reshape.52), calls=%async_computation | async-start | bytes 589824 | tf_op jit(solution)/shard_map/all_to_all | solution.py:296
  56.1 24.2 %all-to-all-start.1 = ((bf16[8,128,640]{2,1,0:T(8,128)(2,1)}), bf16[8,128,640]{2,1,0:T(8,128)(2,1)S(1)}, u32[]{:S(2)}, u32[]{:S(2)}) async-start(bf16[8,128,640]{2,1,0:T(8,128)(2,1)} %broadcast_in_dim.28), calls=%async_computation.1 | async-start | bytes 2621440 | tf_op jit(solution)/shard_map/all_to_all | solution.py:312
  62.5 27.9 %copy-start.6 = (s32[128]{0:T(128)S(1)}, s32[128]{0:T(128)}, u32[]{:S(2)}) copy-start(s32[128]{0:T(128)} %param.20) | copy-start | bytes 1540
  62.5 27.9 %copy-start.7 = (s32[128]{0:T(128)S(1)}, s32[128]{0:T(128)}, u32[]{:S(2)}) copy-start(s32[128]{0:T(128)} %param.21) | copy-start | bytes 1540
  80.3 1.1 copy-start
  85.8 16.4 %all-to-all-start.2 = ((bf16[64,2,256]{2,1,0:T(2,128)(2,1)}), bf16[64,2,256]{2,1,0:T(2,128)(2,1)S(1)}, u32[]{:S(2)}, u32[]{:S(2)}) async-start(bf16[64,2,256]{2,1,0:T(2,128)(2,1)} %reshape.55), calls=%async_computation.2 | async-start | bytes 131072 | tf_op jit(solution)/shard_map/all_to_all | solution.py:320
  116.5 14.6 %copy-start.5 = (bf16[2,128,128]{2,1,0:T(8,128)(2,1)S(1)}, bf16[2,128,128]{2,1,0:T(8,128)(2,1)}, u32[]{:S(2)}) copy-start(bf16[2,128,128]{2,1,0:T(8,128)(2,1)} %param.12) | copy-start | bytes 196612
  125.7 15.5 %all-to-all-start.3 = ((bf16[8,144,256]{2,1,0:T(8,128)(2,1)}), bf16[8,144,256]{2,1,0:T(8,128)(2,1)S(1)}, u32[]{:S(2)}, u32[]{:S(2)}) async-start(bf16[8,144,256]{2,1,0:T(8,128)(2,1)} %shard_map.158), calls=%async_computation.3 | async-start | bytes 1179648 | tf_op jit(solution)/shard_map/all_to_all | solution.py:339
  141.1 0.9 copy-start.1
  146.1 10.8 %all-to-all-start.4 = ((bf16[8,128,128]{2,1,0:T(8,128)(2,1)}), bf16[8,128,128]{2,1,0:T(8,128)(2,1)S(1)}, u32[]{:S(2)}, u32[]{:S(2)}) async-start(bf16[8,128,128]{2,1,0:T(8,128)(2,1)} %get-tuple-element.34), calls=%async_computation.4 | async-start | bytes 524288 | tf_op jit(solution)/shard_map/all_to_all | solution.py:347
  156.9 0.7 copy-start.2
Sparse Core Ops, SparseCore 0:
  11.6 104.8 all-gather.1

commit v2 on v1

--- a/solution.py
+++ b/solution.py
@@ -18,7 +18,7 @@
 CW = 16
 GW = HW + CW
 HP = 2688
-BLK = 384
+BLK = 896
 CONV = 2 * K * NAR
 W1 = 384
 W2 = 1152
@@ -26,11 +26,11 @@
 P2 = 64
 SROW = 16
 NEG = -1e30
+LIMIT = 24 * 2**20
 f32 = jnp.float32
 bf16 = jnp.bfloat16
 VMEM = pl.BlockSpec(memory_space=pltpu.VMEM)
 SMEM = pl.BlockSpec(memory_space=pltpu.SMEM)
-ANY = pl.BlockSpec(memory_space=pl.ANY)
 
 
 def dot(a, b, ca=1, cb=0):
@@ -48,7 +48,7 @@
     return lax.broadcasted_iota(jnp.int32, shape, axis)
 
 
-def call(kernel, outs, *args, specs=None, scratch=(), flops=10**7, nbytes=10**6):
+def call(kernel, outs, *args, specs=None, scratch=(), limit=None, flops=10**7, nbytes=10**6):
     outs = [jax.ShapeDtypeStruct(shape, kind) for shape, kind in outs]
     return pl.pallas_call(
         kernel,
@@ -56,22 +56,35 @@
         in_specs=[VMEM] * len(args) if specs is None else specs,
         out_specs=[VMEM] * len(outs),
         scratch_shapes=list(scratch),
+        compiler_params=pltpu.CompilerParams(vmem_limit_bytes=limit),
         cost_estimate=pl.CostEstimate(flops=flops, bytes_accessed=nbytes, transcendentals=0),
     )(*args)
 
 
-def route_kernel(cid_row, cid_col, tgt_col, hidden, send, pick):
-    owner_row = jnp.where(cid_row[...] >= 0, cid_row[...] // 2, -1)
-    owner_col = jnp.where(cid_col[...] >= 0, cid_col[...] // 2, -2)
+def pack_kernel(head, cluster, conv, out):
+    out[:, :HW] = head[...]
+    out[:, HW:HP] = jnp.zeros((out.shape[0], HP - HW), bf16)
+    out[:, HW:GW] = cluster[...]
+    for half in range(2):
+        for k in range(K):
+            at = HP + (half * K + k) * NAR
+            out[:, at : at + NAR] = conv[half, k]
+
+
+def route_kernel(cid, tgt, hidden, send, pick):
+    cid_row = jnp.broadcast_to(cid[...], (T, T))
+    cid_col = cid_row.astype(f32).T.astype(jnp.int32)
+    word = jnp.broadcast_to(tgt[...], (T, T)).astype(f32).T.astype(jnp.int32)
+    owner_row = jnp.where(cid_row >= 0, cid_row // 2, -1)
+    owner_col = jnp.where(cid_col >= 0, cid_col // 2, -2)
     before = (owner_col == owner_row) & (iota((T, T), 0) < iota((T, T), 1))
     rank = jnp.sum(before.astype(f32), axis=0, keepdims=True).astype(jnp.int32)
     slot = jnp.where(owner_row >= 0, owner_row * 2 + rank, -1)
     chosen = (iota((T, T), 0) == slot).astype(bf16)
     pick[...] = chosen
     send[:, :D] = dot(chosen, hidden[...]).astype(bf16)
-    lane = iota((T, 128), 1)
-    word = tgt_col[...]
-    tier = jnp.where(cid_col[...] >= 0, cid_col[...] % 2 + 1, 0)
+    lane = iota((T, T), 1)
+    tier = jnp.where(cid_col >= 0, cid_col % 2 + 1, 0)
     meta = jnp.where(lane == 0, word // 128, jnp.where(lane == 1, word % 128, jnp.where(lane == 2, tier, 0)))
     send[:, D:] = dot(chosen, meta.astype(f32).astype(bf16)).astype(bf16)
 
@@ -83,11 +96,12 @@
     return word, tier
 
 
-def tail_kernel(ch, rows, meta, proj1, proj2, out1, out2, feat, part):
-    word, tier = slot_meta(meta[...])
+def tail_kernel(ch, got, proj1, proj2, out1, out2, feat, part):
+    word, tier = slot_meta(got[:, D:])
+    rows = got[:, :D]
     first = tier == 1
-    z1 = dot(rows[...], proj1[...])
-    z2 = dot(rows[...], proj2[...])
+    z1 = dot(rows, proj1[...])
+    z2 = dot(rows, proj2[...])
     features = jnp.where(first, z1, z2).astype(bf16)
     feat[...] = features
 
@@ -105,17 +119,21 @@
     one = local(out1, W1)
     two = local(out2, W2)
     top, total, target, value, column = [jnp.where(first, a, b) for a, b in zip(one, two)]
-    part[:, :P1] = value.astype(bf16)
-    part[:, P1 : 2 * P1] = column.astype(bf16)
+    value = value.astype(bf16)
+    column = column.astype(bf16)
     lane = iota((T, 128), 1)
     stats = jnp.zeros((T, 128), f32)
     for i, x in enumerate(parts3(top) + parts3(total) + parts3(target)):
         stats = jnp.where(lane == i, x, stats)
-    part[:, 2 * P1 :] = stats.astype(bf16)
-
-
-def tail_merge_kernel(meta, parts, proj1_part, proj2_part, dz1, dz2, log_total, back):
-    _, tier = slot_meta(meta[...])
+    stats = stats.astype(bf16)
+    for g in range(NCH):
+        part[g, :, :P1] = value
+        part[g, :, P1 : 2 * P1] = column
+        part[g, :, 2 * P1 :] = stats
+
+
+def tail_merge_kernel(ch, got, parts, proj1, proj2, dz1, dz2, log_total, back):
+    _, tier = slot_meta(got[:, D:])
     tops, totals, target = [], [], 0.0
     for g in range(NCH):
         stats = parts[g, :, 2 * P1 :].astype(f32)
@@ -139,7 +157,8 @@
     dz1[...] = one
     dz2[...] = two
     log_total[...] = jnp.broadcast_to(log_all, (T, 128))
-    back[:, :NAR] = (dot(one, proj1_part[...], 1, 1) + dot(two, proj2_part[...], 1, 1)).astype(bf16)
+    mine = pl.ds(pl.multiple_of(ch[0] * NAR, NAR), NAR)
+    back[:, :NAR] = (dot(one, proj1[mine, :], 1, 1) + dot(two, proj2[mine, :], 1, 1)).astype(bf16)
     loss = jnp.where(tier > 0, log_all - target, 0.0)
     lane = iota((T, 128), 1)
     tail = jnp.zeros((T, 128), f32)
@@ -148,8 +167,9 @@
     back[:, NAR:] = tail.astype(bf16)
 
 
-def tail_grad_kernel(ch, meta, feat, rows_part, dz1, dz2, log_total, out1, out2, g_out1, g_out2, g_proj1, g_proj2):
-    word, tier = slot_meta(meta[...])
+def tail_grad_kernel(ch, got, feat, dz1, dz2, log_total, out1, out2, g_out1, g_out2, g_proj1, g_proj2):
+    word, tier = slot_meta(got[:, D:])
+    rows_part = got[:, pl.ds(pl.multiple_of(ch[0] * NAR, NAR), NAR)]
     features = feat[...]
     log_all = log_total[:, 0:1]
 
@@ -160,8 +180,8 @@
 
     g_out1[...] = dot(features, slope(out1, W1, 1), 0, 0)
     g_out2[...] = dot(features, slope(out2, W2, 2), 0, 0)[:P2]
-    g_proj1[...] = dot(rows_part[...], dz1[...], 0, 0)
-    g_proj2[...] = dot(rows_part[...], dz2[...], 0, 0)[:, :P2]
+    g_proj1[...] = dot(rows_part, dz1[...], 0, 0)
+    g_proj2[...] = dot(rows_part, dz2[...], 0, 0)[:, :P2]
 
 
 def back_kernel(got, pick, back_t, loss):
@@ -225,9 +245,7 @@
     )(col, hidden, weight)
 
 
-def conv_kernel(parts, back_t, tail_loss, gates, weight, conv, grad, loss, taps, wide, sem):
-    copy = pltpu.make_async_copy(weight.at[:, pl.ds(HP, CONV)], wide, sem)
-    copy.start()
+def conv_kernel(parts, back_t, tail_loss, gates, weight, conv, grad, loss, taps):
     tops, totals, target = [], [], 0.0
     for g in range(NCH):
         stats = parts[g, NAR:, :T].astype(f32)
@@ -258,8 +276,7 @@
             moved = value if k == 0 else jnp.where(lane < T - k, pltpu.roll(value, T - k, 1), 0.0)
             at = (half * K + k) * NAR
             taps[at : at + NAR, :] = moved.astype(bf16)
-    copy.wait()
-    total_conv = dot(wide[...], taps[...])
+    total_conv = dot(weight[...], taps[...])
     for g in range(NCH):
         conv[g] = total_conv[g * NAR : (g + 1) * NAR].astype(bf16)
 
@@ -274,55 +291,40 @@
 def on_device(hidden, pre_gates, conv_weight, head_weight, cluster_weight, tail1_proj, tail2_proj, tail1_out, tail2_out, cluster_id, target):
     ch = lax.axis_index("ch").astype(jnp.int32)
     ch_arr = ch.reshape(1)
-    packed = jnp.concatenate(
-        [
-            head_weight,
-            cluster_weight,
-            jnp.zeros((head_weight.shape[0], HP - GW), bf16),
-            conv_weight.transpose(2, 0, 1, 3).reshape(head_weight.shape[0], CONV),
-        ],
-        axis=1,
-    )
+    (packed,) = call(pack_kernel, [((head_weight.shape[0], HP + CONV), bf16)], head_weight, cluster_weight, conv_weight)
     gathered = lax.all_gather(packed, "tok", axis=0, tiled=True)
 
     send, pick = call(
         route_kernel,
         [((T, D + 128), bf16), ((T, T), bf16)],
         cluster_id.reshape(1, T),
-        cluster_id.reshape(T, 1),
-        target.reshape(T, 1),
+        target.reshape(1, T),
         hidden,
     )
     got = lax.all_to_all(send.reshape(OWN, 2, D + 128), "tok", split_axis=0, concat_axis=0, tiled=True).reshape(T, D + 128)
-    rows, meta = got[:, :D], got[:, D:]
     proj1 = tail1_proj[0]
     proj2 = jnp.pad(tail2_proj[0], ((0, 0), (0, P1 - P2)))
     out1 = tail1_out[0]
     out2 = jnp.pad(tail2_out[0], ((0, P1 - P2), (0, 0)))
-    col_start = ch * NAR
-    proj1_part = lax.dynamic_slice_in_dim(proj1, col_start, NAR, 0)
-    proj2_part = lax.dynamic_slice_in_dim(proj2, col_start, NAR, 0)
-    rows_part = lax.dynamic_slice_in_dim(rows, col_start, NAR, 1)
     feat, part = call(
         tail_kernel,
-        [((T, P1), bf16), ((T, 2 * P1 + 128), bf16)],
-        ch_arr, rows, meta, proj1, proj2, out1, out2,
-        specs=[SMEM] + [VMEM] * 6,
-    )
-    parts = lax.all_to_all(
-        jnp.broadcast_to(part[None], (NCH,) + part.shape), "ch", split_axis=0, concat_axis=0, tiled=True
-    )
+        [((T, P1), bf16), ((NCH, T, 2 * P1 + 128), bf16)],
+        ch_arr, got, proj1, proj2, out1, out2,
+        specs=[SMEM] + [VMEM] * 5,
+    )
+    parts = lax.all_to_all(part, "ch", split_axis=0, concat_axis=0, tiled=True)
     dz1, dz2, log_total, back = call(
         tail_merge_kernel,
         [((T, P1), bf16), ((T, P1), bf16), ((T, 128), f32), ((T, NAR + 128), bf16)],
-        meta, parts, proj1_part, proj2_part,
+        ch_arr, got, parts, proj1, proj2,
+        specs=[SMEM] + [VMEM] * 4,
     )
     got_back = lax.all_to_all(back.reshape(OWN, 2, NAR + 128), "tok", split_axis=0, concat_axis=0, tiled=True).reshape(T, NAR + 128)
     g_out1, g_out2, g_proj1, g_proj2 = call(
         tail_grad_kernel,
         [((P1, W1), f32), ((P2, W2), f32), ((NAR, P1), f32), ((NAR, P2), f32)],
-        ch_arr, meta, feat, rows_part, dz1, dz2, log_total, out1, out2,
-        specs=[SMEM] + [VMEM] * 8,
+        ch_arr, got, feat, dz1, dz2, log_total, out1, out2,
+        specs=[SMEM] + [VMEM] * 7,
     )
     back_t, tail_loss = call(back_kernel, [((NAR, T), f32), ((1, T), f32)], got_back, pick)
 
@@ -340,12 +342,12 @@
     conv, grad, loss = call(
         conv_kernel,
         [((NCH, NAR, T), bf16), ((NAR, T), f32), ((1, T), f32)],
-        head_parts, back_t, tail_loss, pre_gates.transpose(0, 2, 1), gathered,
-        specs=[VMEM] * 4 + [ANY],
-        scratch=[pltpu.VMEM((CONV, T), bf16), pltpu.VMEM((D, CONV), bf16), pltpu.SemaphoreType.DMA],
+        head_parts, back_t, tail_loss, pre_gates.transpose(0, 2, 1), gathered[:, HP:],
+        scratch=[pltpu.VMEM((CONV, T), bf16)],
+        limit=LIMIT,
     )
     conv_parts = lax.all_to_all(conv, "ch", split_axis=0, concat_axis=0, tiled=True)
-    (grad_input,) = call(final_kernel, [((T, NAR), bf16)], conv_parts, grad)
+    (grad_input,) = call(final_kernel, [((T, NAR), bf16)], conv_parts, grad, limit=LIMIT)
     return (loss.reshape(T), grad_input, g_proj1[None], g_proj2[None], g_out1[None], g_out2[None])
 
 

time: 167 us -> 158 us (0.946)
  local copies, waits for them, and re-layouts: 23.2 us -> 12.2 us
  Pallas kernels: 28.3 us -> 24.7 us
  waiting for transfers between devices: 62.1 us -> 65.7 us
  starting transfers between devices: 37.9 us -> 39.8 us
    all_gather x1, waiting for transfers between devices: 11.9 us -> 16 us  [on_device(): gathered = lax.all_gather(packed, 'tok', axis=0, tiled=True)]
    dynamic_slice x3 -> x0, local copies, waits for them, and re-layouts: 3.49 us -> none  [the longest x1 1.47 us: on_device(): proj1_part = lax.dynamic_slice_in_dim(proj1, col_start, NAR, 0)]
    all_to_all x1, waiting for transfers between devices: 13.2 us -> 10.4 us  [on_device(): lax.all_to_all(send.reshape(OWN, 2, D + 128), 'tok', split_axis=0, concat...]
    reshape x3 -> x0, local copies, waits for them, and re-layouts: 2.79 us -> none  [the longest x1 1.39 us: on_device(): cluster_id.reshape(T, 1)]
    pallas_call x1, Pallas kernels: 9.2 us -> 6.73 us  [head_call(): pl.pallas_call(head_kernel, out_shape=jax.ShapeDtypeStruct((NCH, NAR + SR...]
    broadcast_in_dim x2 -> x0, local copies, waits for them, and re-layouts: 2.14 us -> none  [the longest x1 2.14 us: on_device(): jnp.broadcast_to(part[None], (NCH,) + part.shape)]
    all_to_all x1, waiting for transfers between devices: 15.7 us -> 17.8 us  [on_device(): parts = lax.all_to_all(part, 'ch', split_axis=0, concat_axis=0, tiled=True)]
    all_to_all x1, starting transfers between devices: 6.45 us -> 8.36 us  [on_device(): parts = lax.all_to_all(part, 'ch', split_axis=0, concat_axis=0, tiled=True)]
  transfers between devices with their start and end apart: 6 -> 6, of which waited for: 6 -> 6; matrix products, arithmetic and copies ran while one was open for 11% -> 7% of each run, Pallas kernels for 8% -> 9%
where the time goes in v2:
time: 158 us; the launch traced here: 157 us
  waiting for transfers between devices  65.7 us (42%)
  starting transfers between devices  39.8 us (25%)
  Pallas kernels  24.7 us (16%)
  between operations  14.1 us (9%)
  local copies, waits for them, and re-layouts  12.2 us (8%)
    pallas_call x8, Pallas kernels, call(): pl.pallas_call(kernel, out_shape=outs, in_specs=[VMEM] * len(args) if spe...  18 us
    all_to_all x1, waiting for transfers between devices, on_device(): parts = lax.all_to_all(part, 'ch', split_axis=0, concat_axis=0, tiled=True)  17.8 us
    all_to_all x1, starting transfers between devices, on_device(): lax.all_to_all(send.reshape(OWN, 2, D + 128), 'tok', split_axis=0, concat...  17.1 us
    all_gather x1, waiting for transfers between devices, on_device(): gathered = lax.all_gather(packed, 'tok', axis=0, tiled=True)  16 us
    all_to_all x1, waiting for transfers between devices, on_device(): lax.all_to_all(back.reshape(OWN, 2, NAR + 128), 'tok', split_axis=0, conc...  11.2 us
    all_to_all x1, waiting for transfers between devices, on_device(): lax.all_to_all(send.reshape(OWN, 2, D + 128), 'tok', split_axis=0, concat...  10.4 us
    all_to_all x1, starting transfers between devices, on_device(): parts = lax.all_to_all(part, 'ch', split_axis=0, concat_axis=0, tiled=True)  8.36 us
    all_to_all x1, waiting for transfers between devices, on_device(): lax.all_to_all(head, 'ch', split_axis=0, concat_axis=0, tiled=True)  8.11 us
  transfers between devices with their start and end apart: 6, of which 6 were waited for; matrix products, arithmetic and copies ran while one was open for 7% of the time, Pallas kernels for 9%

profile of v2, /device:TPU:1, one launch (start us, length us, event | category | flops | bytes accessed | tf_op | source)
XLA Modules:
  0.0 157.1 jit_solution(1000585794710373033)
XLA Ops:
  7.2 1.6 %shard_map.154 = bf16[16,3712]{1,0:T(8,128)(2,1)} custom-call(bf16[16,2560]{1,0:T(8,128)(2,1)} %head.1, bf16[16,16]{1,0:T(8,128)(2,1)} %cluster.1, bf16[2,4,16,128]{3,2,1,0:T(8,128)(2,1)} %conv.1), custom_call_target="tpu_custom_call" | custom-call | flops 10000000 | bytes 1000000 | tf_op jit(solution)/shard_map/pallas_call | solution.py:53
  8.8 2.1 %shard_map.155 = (bf16[128,1152]{1,0:T(8,128)(2,1)}, bf16[128,128]{1,0:T(8,128)(2,1)}) custom-call(s32[1,128]{1,0:T(1,128)} %bitcast.24, s32[1,128]{1,0:T(1,128)} %bitcast.23, bf16[128,1024]{1,0:T(8,128)(2,1)} %hidden.3), custom_call_target="tpu_custom_call" | custom-call | flops 10000000 | bytes 1000000 | tf_op jit(solution)/shard_map/pallas_call | solution.py:53
  11.0 1.8 %reshape.43 = bf16[64,2,1152]{2,1,0:T(2,128)(2,1)} reshape(bf16[128,1152]{1,0:T(8,128)(2,1)} %get-tuple-element.25) | data formatting | bytes 589824 | tf_op jit(solution)/shard_map/reshape | solution.py:304
  12.7 17.1 %all-to-all-start = ((bf16[64,2,1152]{2,1,0:T(2,128)(2,1)}), bf16[64,2,1152]{2,1,0:T(2,128)(2,1)S(1)}, u32[]{:S(2)}, u32[]{:S(2)}) async-start(bf16[64,2,1152]{2,1,0:T(2,128)(2,1)} %reshape.43), calls=%async_computation | async-start | bytes 589824 | tf_op jit(solution)/shard_map/all_to_all | solution.py:304
  29.9 1.1 copy.17
  31.0 0.9 pad.8.proj2
  31.8 0.9 pad.9.out2
  32.7 10.4 %all-to-all-done = bf16[64,2,1152]{2,1,0:T(2,128)(2,1)S(1)} async-done(((bf16[64,2,1152]{2,1,0:T(2,128)(2,1)}), bf16[64,2,1152]{2,1,0:T(2,128)(2,1)S(1)}, u32[]{:S(2)}, u32[]{:S(2)}) %all-to-all-start) | async-done | bytes 294944 | tf_op jit(solution)/shard_map/all_to_all | solution.py:304
  43.1 0.8 reshape.44.got
  43.9 4.2 %shard_map.156 = (bf16[128,256]{1,0:T(8,128)(2,1)}, bf16[8,128,640]{2,1,0:T(8,128)(2,1)}) custom-call(s32[1]{0:T(128)} %bitcast.1.ch, bf16[128,1152]{1,0:T(8,128)(2,1)} %reshape.44.got, bf16[1024,256]{1,0:T(8,128)(2,1)} %bitcast.16, bf16[1024,256]{1,0:T(8,128)(2,1)} %pad.8.proj2, bf16[256,384]{1,0:T(8,128)(2,1)} %bitcast.19, bf16[256,1152]{1,0:T(8,128)(2,1)} %pad.9.out2), custom_call_target="tpu_custom_call" | custom-call | flops 10000000 | bytes 1000000 | tf_op jit(solution)/shard_map/pallas_call | solution.py:53
  48.1 8.4 %all-to-all-start.1 = ((bf16[8,128,640]{2,1,0:T(8,128)(2,1)}), bf16[8,128,640]{2,1,0:T(8,128)(2,1)S(1)}, u32[]{:S(2)}, u32[]{:S(2)}) async-start(bf16[8,128,640]{2,1,0:T(8,128)(2,1)} %get-tuple-element.26), calls=%async_computation.1 | async-start | bytes 2621440 | tf_op jit(solution)/shard_map/all_to_all | solution.py:315
  56.5 17.8 %all-to-all-done.1.parts = bf16[8,128,640]{2,1,0:T(8,128)(2,1)S(1)} async-done(((bf16[8,128,640]{2,1,0:T(8,128)(2,1)}), bf16[8,128,640]{2,1,0:T(8,128)(2,1)S(1)}, u32[]{:S(2)}, u32[]{:S(2)}) %all-to-all-start.1) | async-done | bytes 1310752 | tf_op jit(solution)/shard_map/all_to_all | solution.py:315
  74.3 1.1 copy-done.2
  75.4 3.2 %shard_map.157 = (bf16[128,256]{1,0:T(8,128)(2,1)}, bf16[128,256]{1,0:T(8,128)(2,1)}, f32[128,128]{1,0:T(8,128)}, bf16[128,256]{1,0:T(8,128)(2,1)}) custom-call(s32[1]{0:T(128)} %bitcast.1.ch, bf16[128,1152]{1,0:T(8,128)(2,1)} %reshape.44.got, bf16[8,128,640]{2,1,0:T(8,128)(2,1)} %copy-done.2, bf16[1024,256]{1,0:T(8,128)(2,1)} %bitcast.17, ...), custom_call_target="tpu_custom_call" | custom-call | flops 10000000 | bytes 1000000 | tf_op jit(solution)/shard_map/pallas_call | solution.py:53
  78.6 1.5 reshape.45
  80.1 4.6 %all-to-all-start.2 = ((bf16[64,2,256]{2,1,0:T(2,128)(2,1)}), bf16[64,2,256]{2,1,0:T(2,128)(2,1)S(1)}, u32[]{:S(2)}, u32[]{:S(2)}) async-start(bf16[64,2,256]{2,1,0:T(2,128)(2,1)} %reshape.45), calls=%async_computation.2 | async-start | bytes 131072 | tf_op jit(solution)/shard_map/all_to_all | solution.py:322
  84.8 0.5 fusion.col
  85.3 11.2 %all-to-all-done.2 = bf16[64,2,256]{2,1,0:T(2,128)(2,1)S(1)} async-done(((bf16[64,2,256]{2,1,0:T(2,128)(2,1)}), bf16[64,2,256]{2,1,0:T(2,128)(2,1)S(1)}, u32[]{:S(2)}, u32[]{:S(2)}) %all-to-all-start.2) | async-done | bytes 65568 | tf_op jit(solution)/shard_map/all_to_all | solution.py:322
  96.5 0.7 reshape.46.got
  97.2 1.7 %shard_map.158 = (f32[128,128]{1,0:T(8,128)}, f32[1,128]{1,0:T(1,128)}) custom-call(bf16[128,256]{1,0:T(8,128)(2,1)} %reshape.46.got, bf16[128,128]{1,0:T(8,128)(2,1)} %get-tuple-element.28.pick), custom_call_target="tpu_custom_call" | custom-call | flops 10000000 | bytes 1000000 | tf_op jit(solution)/shard_map/pallas_call | solution.py:53
  98.8 16.0 %all-gather.2.cloned.1.call-done.weight = bf16[1024,3712]{1,0:T(8,128)(2,1)} async-done(((bf16[16,3712]{1,0:T(8,128)(2,1)}), bf16[1024,3712]{1,0:T(8,128)(2,1)}) %all-gather.2.cloned.1.call-update) | async-done | bytes 7602192 | tf_op jit(solution)/shard_map/all_gather | solution.py:295
  114.9 6.7 %shard_map.159 = bf16[8,144,256]{2,1,0:T(8,128)(2,1)} custom-call(s32[1,128]{1,0:T(1,128)} %fusion.col, bf16[128,1024]{1,0:T(8,128)(2,1)} %hidden.3, bf16[1024,3712]{1,0:T(8,128)(2,1)} %all-gather.2.cloned.1.call-done.weight), custom_call_target="tpu_custom_call" | custom-call | flops 2000000000 | bytes 6000000 | tf_op jit(solution)/shard_map/pallas_call | solution.py:232
  121.6 5.4 %all-to-all-start.3 = ((bf16[8,144,256]{2,1,0:T(8,128)(2,1)}), bf16[8,144,256]{2,1,0:T(8,128)(2,1)S(1)}, u32[]{:S(2)}, u32[]{:S(2)}) async-start(bf16[8,144,256]{2,1,0:T(8,128)(2,1)} %shard_map.159), calls=%async_computation.3 | async-start | bytes 1179648 | tf_op jit(solution)/shard_map/all_to_all | solution.py:341
  127.0 0.1 copy.18
  127.2 1.8 %slice.3.weight = bf16[1024,1024]{1,0:T(8,128)(2,1)S(1)} slice(bf16[1024,3712]{1,0:T(8,128)(2,1)} %all-gather.2.cloned.1.call-done.weight), slice={[0:1024], [2688:3712]} | slice | bytes 4194304 | tf_op jit(solution)/shard_map/slice | solution.py:345
  129.0 8.1 %all-to-all-done.3.parts = bf16[8,144,256]{2,1,0:T(8,128)(2,1)S(1)} async-done(((bf16[8,144,256]{2,1,0:T(8,128)(2,1)}), bf16[8,144,256]{2,1,0:T(8,128)(2,1)S(1)}, u32[]{:S(2)}, u32[]{:S(2)}) %all-to-all-start.3) | async-done | bytes 589856 | tf_op jit(solution)/shard_map/all_to_all | solution.py:341
  137.1 1.6 %shard_map.160 = (bf16[8,128,128]{2,1,0:T(8,128)(2,1)}, f32[128,128]{1,0:T(8,128)S(1)}, f32[1,128]{1,0:T(1,128)}) custom-call(bf16[8,144,256]{2,1,0:T(8,128)(2,1)S(1)} %all-to-all-done.3.parts, f32[128,128]{1,0:T(8,128)S(1)} %copy-done, f32[1,128]{1,0:T(1,128)S(1)} %copy-done.1, bf16[2,128,128]{2,1,0:T(8,128)(2,1)S(1)} %bitcast.15, ...), custom_call_target="tpu_custom_call" | custom-call | flops 10000000 | bytes 1000000 | tf_op jit(solution)/shard_map/pallas_call | solution.py:53
  138.7 4.3 %all-to-all-start.4 = ((bf16[8,128,128]{2,1,0:T(8,128)(2,1)}), bf16[8,128,128]{2,1,0:T(8,128)(2,1)S(1)}, u32[]{:S(2)}, u32[]{:S(2)}) async-start(bf16[8,128,128]{2,1,0:T(8,128)(2,1)} %get-tuple-element.34), calls=%async_computation.4 | async-start | bytes 524288 | tf_op jit(solution)/shard_map/all_to_all | solution.py:349
  143.0 2.8 %shard_map.162 = (f32[256,384]{1,0:T(8,128)}, f32[64,1152]{1,0:T(8,128)}, f32[128,256]{1,0:T(8,128)}, f32[128,64]{1,0:T(8,128)}) custom-call(s32[1]{0:T(128)} %bitcast.1.ch, bf16[128,1152]{1,0:T(8,128)(2,1)} %reshape.44.got, bf16[128,256]{1,0:T(8,128)(2,1)} %get-tuple-element.36.feat, bf16[128,256]{1,0:T(8,128)(2,1)} %get-tuple-element.37.dz1, ...), custom_call_target="tpu_custom_call" | custom-call | flops 10000000 | bytes 1000000 | tf_op jit(solution)/shard_map/pallas_call | solution.py:53
  145.8 1.5 copy.19
  147.3 2.2 %all-to-all-done.4.parts = bf16[8,128,128]{2,1,0:T(8,128)(2,1)S(1)} async-done(((bf16[8,128,128]{2,1,0:T(8,128)(2,1)}), bf16[8,128,128]{2,1,0:T(8,128)(2,1)S(1)}, u32[]{:S(2)}, u32[]{:S(2)}) %all-to-all-start.4) | async-done | bytes 262176 | tf_op jit(solution)/shard_map/all_to_all | solution.py:349
  149.5 0.7 shard_map.161
  (15 shorter events, 0.1 us)
Async XLA Ops:
  7.2 24.7 %copy-start.3 = (bf16[1,64,1152]{2,1,0:T(8,128)(2,1)S(1)}, bf16[1,64,1152]{2,1,0:T(8,128)(2,1)}, u32[]{:S(2)}) copy-start(bf16[1,64,1152]{2,1,0:T(8,128)(2,1)} %param.19) | copy-start | bytes 442372
  7.2 107.7 %all-gather.2.cloned.1.call-start = ((), (), s32[]{:S(2)}) async-start(), calls=%async_computation.5 | async-start | bytes 7720960 | tf_op jit(solution)/shard_map/all_gather | solution.py:295
  12.7 30.3 %all-to-all-start = ((bf16[64,2,1152]{2,1,0:T(2,128)(2,1)}), bf16[64,2,1152]{2,1,0:T(2,128)(2,1)S(1)}, u32[]{:S(2)}, u32[]{:S(2)}) async-start(bf16[64,2,1152]{2,1,0:T(2,128)(2,1)} %reshape.43), calls=%async_computation | async-start | bytes 589824 | tf_op jit(solution)/shard_map/all_to_all | solution.py:304
  48.1 26.1 %all-to-all-start.1 = ((bf16[8,128,640]{2,1,0:T(8,128)(2,1)}), bf16[8,128,640]{2,1,0:T(8,128)(2,1)S(1)}, u32[]{:S(2)}, u32[]{:S(2)}) async-start(bf16[8,128,640]{2,1,0:T(8,128)(2,1)} %get-tuple-element.26), calls=%async_computation.1 | async-start | bytes 2621440 | tf_op jit(solution)/shard_map/all_to_all | solution.py:315
  56.5 28.3 %copy-start.5 = (s32[128]{0:T(128)S(1)}, s32[128]{0:T(128)}, u32[]{:S(2)}) copy-start(s32[128]{0:T(128)} %param.21) | copy-start | bytes 1540
  56.5 28.3 %copy-start.6 = (s32[128]{0:T(128)S(1)}, s32[128]{0:T(128)}, u32[]{:S(2)}) copy-start(s32[128]{0:T(128)} %param.20) | copy-start | bytes 1540
  74.3 1.1 copy-start.2
  80.1 16.4 %all-to-all-start.2 = ((bf16[64,2,256]{2,1,0:T(2,128)(2,1)}), bf16[64,2,256]{2,1,0:T(2,128)(2,1)S(1)}, u32[]{:S(2)}, u32[]{:S(2)}) async-start(bf16[64,2,256]{2,1,0:T(2,128)(2,1)} %reshape.45), calls=%async_computation.2 | async-start | bytes 131072 | tf_op jit(solution)/shard_map/all_to_all | solution.py:322
  114.9 12.1 %copy-start.4 = (bf16[2,128,128]{2,1,0:T(8,128)(2,1)S(1)}, bf16[2,128,128]{2,1,0:T(8,128)(2,1)}, u32[]{:S(2)}) copy-start(bf16[2,128,128]{2,1,0:T(8,128)(2,1)} %param.12) | copy-start | bytes 196612
  121.6 15.5 %all-to-all-start.3 = ((bf16[8,144,256]{2,1,0:T(8,128)(2,1)}), bf16[8,144,256]{2,1,0:T(8,128)(2,1)S(1)}, u32[]{:S(2)}, u32[]{:S(2)}) async-start(bf16[8,144,256]{2,1,0:T(8,128)(2,1)} %shard_map.159), calls=%async_computation.3 | async-start | bytes 1179648 | tf_op jit(solution)/shard_map/all_to_all | solution.py:341
  127.1 9.9 %copy-start = (f32[128,128]{1,0:T(8,128)S(1)}, f32[128,128]{1,0:T(8,128)}, u32[]{:S(2)}) copy-start(f32[128,128]{1,0:T(8,128)} %get-tuple-element.31.back_t) | copy-start | bytes 196612
  127.1 9.9 %copy-start.1 = (f32[1,128]{1,0:T(1,128)S(1)}, f32[1,128]{1,0:T(1,128)}, u32[]{:S(2)}) copy-start(f32[1,128]{1,0:T(1,128)} %get-tuple-element.32.tail_loss) | copy-start | bytes 1540
  138.7 10.8 %all-to-all-start.4 = ((bf16[8,128,128]{2,1,0:T(8,128)(2,1)}), bf16[8,128,128]{2,1,0:T(8,128)(2,1)S(1)}, u32[]{:S(2)}, u32[]{:S(2)}) async-start(bf16[8,128,128]{2,1,0:T(8,128)(2,1)} %get-tuple-element.34), calls=%async_computation.4 | async-start | bytes 524288 | tf_op jit(solution)/shard_map/all_to_all | solution.py:349
Sparse Core Ops, SparseCore 0:
  11.6 103.2 all-gather.1

commit v3 on v2

--- a/solution.py
+++ b/solution.py
@@ -71,7 +71,7 @@
             out[:, at : at + NAR] = conv[half, k]
 
 
-def route_kernel(cid, tgt, hidden, send, pick):
+def route_kernel(ch, cid, tgt, hidden, send, pick):
     cid_row = jnp.broadcast_to(cid[...], (T, T))
     cid_col = cid_row.astype(f32).T.astype(jnp.int32)
     word = jnp.broadcast_to(tgt[...], (T, T)).astype(f32).T.astype(jnp.int32)
@@ -82,11 +82,12 @@
     slot = jnp.where(owner_row >= 0, owner_row * 2 + rank, -1)
     chosen = (iota((T, T), 0) == slot).astype(bf16)
     pick[...] = chosen
-    send[:, :D] = dot(chosen, hidden[...]).astype(bf16)
+    mine = pl.ds(pl.multiple_of(ch[0] * NAR, NAR), NAR)
+    send[:, :NAR] = dot(chosen, hidden[:, mine]).astype(bf16)
     lane = iota((T, T), 1)
     tier = jnp.where(cid_col >= 0, cid_col % 2 + 1, 0)
     meta = jnp.where(lane == 0, word // 128, jnp.where(lane == 1, word % 128, jnp.where(lane == 2, tier, 0)))
-    send[:, D:] = dot(chosen, meta.astype(f32).astype(bf16)).astype(bf16)
+    send[:, NAR:] = dot(chosen, meta.astype(f32).astype(bf16)).astype(bf16)
 
 
 def slot_meta(meta):
@@ -96,17 +97,18 @@
     return word, tier
 
 
-def tail_kernel(ch, got, proj1, proj2, out1, out2, feat, part):
-    word, tier = slot_meta(got[:, D:])
-    rows = got[:, :D]
+def tail_kernel(ch, got, row_parts, proj1, proj2, out1, out2, feat, part, wide):
+    word, tier = slot_meta(got[:, NAR:])
+    rows = jnp.concatenate([row_parts[g] for g in range(NCH)], axis=1)
     first = tier == 1
     z1 = dot(rows, proj1[...])
-    z2 = dot(rows, proj2[...])
-    features = jnp.where(first, z1, z2).astype(bf16)
+    wide[...] = jnp.zeros_like(wide)
+    wide[0, :, :P2] = dot(rows, proj2[...], 1, 1)
+    features = jnp.where(first, z1, wide[0]).astype(bf16)
     feat[...] = features
 
     def local(out, width):
-        logits = dot(features, out[...])
+        logits = dot(feat[:, : out.shape[0]], out[...])
         top = jnp.max(logits, axis=1, keepdims=True)
         terms = jnp.exp(logits - top)
         total = jnp.sum(terms, axis=1, keepdims=True)
@@ -117,7 +119,10 @@
         return top, total, target, value, column
 
     one = local(out1, W1)
-    two = local(out2, W2)
+    two = list(local(out2, W2))
+    for i in (1, 2):
+        wide[i, :, :P2] = two[2 + i]
+        two[2 + i] = wide[i]
     top, total, target, value, column = [jnp.where(first, a, b) for a, b in zip(one, two)]
     value = value.astype(bf16)
     column = column.astype(bf16)
@@ -133,7 +138,7 @@
 
 
 def tail_merge_kernel(ch, got, parts, proj1, proj2, dz1, dz2, log_total, back):
-    _, tier = slot_meta(got[:, D:])
+    _, tier = slot_meta(got[:, NAR:])
     tops, totals, target = [], [], 0.0
     for g in range(NCH):
         stats = parts[g, :, 2 * P1 :].astype(f32)
@@ -158,7 +163,7 @@
     dz2[...] = two
     log_total[...] = jnp.broadcast_to(log_all, (T, 128))
     mine = pl.ds(pl.multiple_of(ch[0] * NAR, NAR), NAR)
-    back[:, :NAR] = (dot(one, proj1[mine, :], 1, 1) + dot(two, proj2[mine, :], 1, 1)).astype(bf16)
+    back[:, :NAR] = (dot(one, proj1[mine, :], 1, 1) + dot(two[:, :P2], proj2[:, mine])).astype(bf16)
     loss = jnp.where(tier > 0, log_all - target, 0.0)
     lane = iota((T, 128), 1)
     tail = jnp.zeros((T, 128), f32)
@@ -168,20 +173,20 @@
 
 
 def tail_grad_kernel(ch, got, feat, dz1, dz2, log_total, out1, out2, g_out1, g_out2, g_proj1, g_proj2):
-    word, tier = slot_meta(got[:, D:])
-    rows_part = got[:, pl.ds(pl.multiple_of(ch[0] * NAR, NAR), NAR)]
+    word, tier = slot_meta(got[:, NAR:])
+    rows_part = got[:, :NAR]
     features = feat[...]
     log_all = log_total[:, 0:1]
 
     def slope(out, width, which):
-        logits = dot(features, out[...])
+        logits = dot(feat[:, : out.shape[0]], out[...])
         hot = (iota((T, width), 1) == word - ch[0] * width).astype(f32)
         return jnp.where(tier == which, jnp.exp(logits - log_all) - hot, 0.0).astype(bf16)
 
     g_out1[...] = dot(features, slope(out1, W1, 1), 0, 0)
-    g_out2[...] = dot(features, slope(out2, W2, 2), 0, 0)[:P2]
+    g_out2[...] = dot(feat[:, :P2], slope(out2, W2, 2), 0, 0)
     g_proj1[...] = dot(rows_part, dz1[...], 0, 0)
-    g_proj2[...] = dot(rows_part, dz2[...], 0, 0)[:, :P2]
+    g_proj2[...] = dot(dz2[:, :P2], rows_part, 0, 0)
 
 
 def back_kernel(got, pick, back_t, loss):
@@ -296,21 +301,25 @@
 
     send, pick = call(
         route_kernel,
-        [((T, D + 128), bf16), ((T, T), bf16)],
+        [((T, NAR + 128), bf16), ((T, T), bf16)],
+        ch_arr,
         cluster_id.reshape(1, T),
         target.reshape(1, T),
         hidden,
-    )
-    got = lax.all_to_all(send.reshape(OWN, 2, D + 128), "tok", split_axis=0, concat_axis=0, tiled=True).reshape(T, D + 128)
+        specs=[SMEM] + [VMEM] * 3,
+    )
+    got = lax.all_to_all(send.reshape(OWN, 2, NAR + 128), "tok", split_axis=0, concat_axis=0, tiled=True).reshape(T, NAR + 128)
+    row_parts = lax.all_gather(got[:, :NAR], "ch")
     proj1 = tail1_proj[0]
-    proj2 = jnp.pad(tail2_proj[0], ((0, 0), (0, P1 - P2)))
+    proj2 = tail2_proj[0].T
     out1 = tail1_out[0]
-    out2 = jnp.pad(tail2_out[0], ((0, P1 - P2), (0, 0)))
+    out2 = tail2_out[0]
     feat, part = call(
         tail_kernel,
         [((T, P1), bf16), ((NCH, T, 2 * P1 + 128), bf16)],
-        ch_arr, got, proj1, proj2, out1, out2,
-        specs=[SMEM] + [VMEM] * 5,
+        ch_arr, got, row_parts, proj1, proj2, out1, out2,
+        specs=[SMEM] + [VMEM] * 6,
+        scratch=[pltpu.VMEM((3, T, P1), f32)],
     )
     parts = lax.all_to_all(part, "ch", split_axis=0, concat_axis=0, tiled=True)
     dz1, dz2, log_total, back = call(
@@ -322,7 +331,7 @@
     got_back = lax.all_to_all(back.reshape(OWN, 2, NAR + 128), "tok", split_axis=0, concat_axis=0, tiled=True).reshape(T, NAR + 128)
     g_out1, g_out2, g_proj1, g_proj2 = call(
         tail_grad_kernel,
-        [((P1, W1), f32), ((P2, W2), f32), ((NAR, P1), f32), ((NAR, P2), f32)],
+        [((P1, W1), f32), ((P2, W2), f32), ((NAR, P1), f32), ((P2, NAR), f32)],
         ch_arr, got, feat, dz1, dz2, log_total, out1, out2,
         specs=[SMEM] + [VMEM] * 7,
     )
@@ -348,7 +357,7 @@
     )
     conv_parts = lax.all_to_all(conv, "ch", split_axis=0, concat_axis=0, tiled=True)
     (grad_input,) = call(final_kernel, [((T, NAR), bf16)], conv_parts, grad, limit=LIMIT)
-    return (loss.reshape(T), grad_input, g_proj1[None], g_proj2[None], g_out1[None], g_out2[None])
+    return (loss.reshape(T), grad_input, g_proj1[None], g_proj2.T[None], g_out1[None], g_out2[None])
 
 
 def solution(mesh):

time: 158 us -> 157 us (level)
  blocking collectives: 0 us -> 44.2 us
  starting transfers between devices: 39.8 us -> 18.3 us
  waiting for transfers between devices: 65.7 us -> 48.9 us
  local copies, waits for them, and re-layouts: 12.2 us -> 6.14 us
    all_to_all x0 -> x1, blocking collectives: none -> 28 us  [on_device(): lax.all_to_all(send.reshape(OWN, 2, NAR + 128), 'tok', split_axis=0, conc...]
    all_to_all x1 -> x0, starting transfers between devices: 17.1 us -> none  [on_device(): lax.all_to_all(send.reshape(OWN, 2, D + 128), 'tok', split_axis=0, concat...]
    all_gather x0 -> x1, blocking collectives: none -> 16.2 us  [on_device(): row_parts = lax.all_gather(got[:, :NAR], 'ch')]
    all_to_all x1 -> x0, waiting for transfers between devices: 10.4 us -> none  [on_device(): lax.all_to_all(send.reshape(OWN, 2, D + 128), 'tok', split_axis=0, concat...]
    all_gather x1, waiting for transfers between devices: 16 us -> 7.86 us  [on_device(): gathered = lax.all_gather(packed, 'tok', axis=0, tiled=True)]
    all_to_all x1, starting transfers between devices: 8.36 us -> 3.99 us  [on_device(): parts = lax.all_to_all(part, 'ch', split_axis=0, concat_axis=0, tiled=True)]
    unnamed x17 -> x15, local copies, waits for them, and re-layouts: 3.88 us -> 1.28 us
    all_to_all x1, waiting for transfers between devices: 2.16 us -> 3.94 us  [on_device(): lax.all_to_all(conv, 'ch', split_axis=0, concat_axis=0, tiled=True)]
  transfers between devices with their start and end apart: 6 -> 5, of which waited for: 6 -> 5; matrix products, arithmetic and copies ran while one was open for 7% -> 4% of each run, Pallas kernels for 9% -> 8%
where the time goes in v3:
time: 157 us; the launch traced here: 156 us
  waiting for transfers between devices  48.9 us (31%)
  blocking collectives  44.2 us (28%)
  Pallas kernels  23.8 us (15%)
  starting transfers between devices  18.3 us (12%)
  between operations  14.1 us (9%)
  local copies, waits for them, and re-layouts  6.14 us (4%)
    all_to_all x1, blocking collectives, on_device(): lax.all_to_all(send.reshape(OWN, 2, NAR + 128), 'tok', split_axis=0, conc...  28 us
    all_to_all x1, waiting for transfers between devices, on_device(): parts = lax.all_to_all(part, 'ch', split_axis=0, concat_axis=0, tiled=True)  17.8 us
    pallas_call x8, Pallas kernels, call(): pl.pallas_call(kernel, out_shape=outs, in_specs=[VMEM] * len(args) if spe...  17.1 us
    all_gather x1, blocking collectives, on_device(): row_parts = lax.all_gather(got[:, :NAR], 'ch')  16.2 us
    all_to_all x1, waiting for transfers between devices, on_device(): lax.all_to_all(back.reshape(OWN, 2, NAR + 128), 'tok', split_axis=0, conc...  11.2 us
    all_to_all x1, waiting for transfers between devices, on_device(): lax.all_to_all(head, 'ch', split_axis=0, concat_axis=0, tiled=True)  8.11 us
    all_gather x1, waiting for transfers between devices, on_device(): gathered = lax.all_gather(packed, 'tok', axis=0, tiled=True)  7.86 us
    pallas_call x1, Pallas kernels, head_call(): pl.pallas_call(head_kernel, out_shape=jax.ShapeDtypeStruct((NCH, NAR + SR...  6.74 us
  transfers between devices with their start and end apart: 5, of which 5 were waited for; matrix products, arithmetic and copies ran while one was open for 4% of the time, Pallas kernels for 8%

profile of v3, /device:TPU:1, one launch (start us, length us, event | category | flops | bytes accessed | tf_op | source)
XLA Modules:
  0.0 156.0 jit_solution(17011646369362169231)
XLA Ops:
  7.2 0.0 all-gather.3.cloned.1.call-start
  7.2 1.6 %shard_map.154 = bf16[16,3712]{1,0:T(8,128)(2,1)} custom-call(bf16[16,2560]{1,0:T(8,128)(2,1)} %head.1, bf16[16,16]{1,0:T(8,128)(2,1)} %cluster.1, bf16[2,4,16,128]{3,2,1,0:T(8,128)(2,1)} %conv.1), custom_call_target="tpu_custom_call" | custom-call | flops 10000000 | bytes 1000000 | tf_op jit(solution)/shard_map/pallas_call | solution.py:53
  8.8 0.0 all-gather.3.cloned.1.call-update
  8.8 2.0 %shard_map.155 = (bf16[128,256]{1,0:T(8,128)(2,1)}, bf16[128,128]{1,0:T(8,128)(2,1)}) custom-call(s32[1]{0:T(128)} %bitcast.1.ch, s32[1,128]{1,0:T(1,128)} %bitcast.31, s32[1,128]{1,0:T(1,128)} %bitcast.30, bf16[128,1024]{1,0:T(8,128)(2,1)} %hidden.3), custom_call_target="tpu_custom_call" | custom-call | flops 10000000 | bytes 1000000 | tf_op jit(solution)/shard_map/pallas_call | solution.py:53
  10.8 0.9 reshape.43
  11.7 28.0 %all_to_all.25 = bf16[64,2,256]{2,1,0:T(2,128)(2,1)S(1)} all-to-all(bf16[64,2,256]{2,1,0:T(2,128)(2,1)S(1)} %reshape.43), channel_id=1, replica_groups=mesh['tok'=64,'ch'=8] {'tok'}, dimensions={0} | all-to-all | bytes 131072 | tf_op jit(solution)/shard_map/all_to_all | solution.py:311
  39.7 0.0 copy-start.3
  39.7 16.2 %all-gather = bf16[1024,128]{1,0:T(8,128)(2,1)} all-gather(bf16[128,128]{1,0:T(8,128)(2,1)S(1)} %slice.8), channel_id=2, replica_groups=mesh['tok'=64,'ch'=8] {'ch'}, dimensions={0}, use_global_device_ids=true | all-gather | bytes 294912 | tf_op jit(solution)/shard_map/all_gather | solution.py:312
  55.9 3.9 %shard_map.156 = (bf16[128,256]{1,0:T(8,128)(2,1)}, bf16[8,128,640]{2,1,0:T(8,128)(2,1)}) custom-call(s32[1]{0:T(128)} %bitcast.1.ch, bf16[128,256]{1,0:T(8,128)(2,1)} %copy-done.3, bf16[8,128,128]{2,1,0:T(8,128)(2,1)} %bitcast.23, bf16[1024,256]{1,0:T(8,128)(2,1)} %bitcast.21, bf16[64,1024]{1,0:T(8,128)(2,1)} %bitcast.28, bf16[256,384]{1,0:T(8,128)(2,1)} %bitcast.24, ...), custom_call_target="tpu_custom_call" | custom-call | flops 10000000 | bytes 1000000 | tf_op jit(solution)/shard_map/pallas_call | solution.py:53
  59.8 4.0 %all-to-all-start.1 = ((bf16[8,128,640]{2,1,0:T(8,128)(2,1)}), bf16[8,128,640]{2,1,0:T(8,128)(2,1)S(1)}, u32[]{:S(2)}, u32[]{:S(2)}) async-start(bf16[8,128,640]{2,1,0:T(8,128)(2,1)} %get-tuple-element.26), calls=%async_computation.1 | async-start | bytes 2621440 | tf_op jit(solution)/shard_map/all_to_all | solution.py:324
  63.8 17.8 %all-to-all-done.1.parts = bf16[8,128,640]{2,1,0:T(8,128)(2,1)S(1)} async-done(((bf16[8,128,640]{2,1,0:T(8,128)(2,1)}), bf16[8,128,640]{2,1,0:T(8,128)(2,1)S(1)}, u32[]{:S(2)}, u32[]{:S(2)}) %all-to-all-start.1) | async-done | bytes 1310752 | tf_op jit(solution)/shard_map/all_to_all | solution.py:324
  81.6 1.1 copy-done.2
  82.7 3.1 %shard_map.157 = (bf16[128,256]{1,0:T(8,128)(2,1)}, bf16[128,256]{1,0:T(8,128)(2,1)}, f32[128,128]{1,0:T(8,128)}, bf16[128,256]{1,0:T(8,128)(2,1)}) custom-call(s32[1]{0:T(128)} %bitcast.1.ch, bf16[128,256]{1,0:T(8,128)(2,1)} %copy-done.3, bf16[8,128,640]{2,1,0:T(8,128)(2,1)} %copy-done.2, bf16[1024,256]{1,0:T(8,128)(2,1)} %bitcast.22, bf16[64,1024]{1,0:T(8,128)(2,1)} %bitcast.29), custom_call_target="tpu_custom_call" | custom-call | flops 10000000 | bytes 1000000 | tf_op jit(solution)/shard_map/pallas_call | solution.py:53
  85.8 1.5 reshape.45
  87.3 4.6 %all-to-all-start.2 = ((bf16[64,2,256]{2,1,0:T(2,128)(2,1)}), bf16[64,2,256]{2,1,0:T(2,128)(2,1)S(1)}, u32[]{:S(2)}, u32[]{:S(2)}) async-start(bf16[64,2,256]{2,1,0:T(2,128)(2,1)} %reshape.45), calls=%async_computation.2 | async-start | bytes 131072 | tf_op jit(solution)/shard_map/all_to_all | solution.py:331
  91.9 0.5 fusion.col
  92.5 11.2 %all-to-all-done.2 = bf16[64,2,256]{2,1,0:T(2,128)(2,1)S(1)} async-done(((bf16[64,2,256]{2,1,0:T(2,128)(2,1)}), bf16[64,2,256]{2,1,0:T(2,128)(2,1)S(1)}, u32[]{:S(2)}, u32[]{:S(2)}) %all-to-all-start.2) | async-done | bytes 65568 | tf_op jit(solution)/shard_map/all_to_all | solution.py:331
  103.7 0.7 reshape.46.got
  104.3 1.7 %shard_map.158 = (f32[128,128]{1,0:T(8,128)}, f32[1,128]{1,0:T(1,128)}) custom-call(bf16[128,256]{1,0:T(8,128)(2,1)} %reshape.46.got, bf16[128,128]{1,0:T(8,128)(2,1)} %get-tuple-element.28.pick), custom_call_target="tpu_custom_call" | custom-call | flops 10000000 | bytes 1000000 | tf_op jit(solution)/shard_map/pallas_call | solution.py:53
  106.0 7.9 %all-gather.3.cloned.1.call-done.weight = bf16[1024,3712]{1,0:T(8,128)(2,1)} async-done(((bf16[16,3712]{1,0:T(8,128)(2,1)}), bf16[1024,3712]{1,0:T(8,128)(2,1)}) %all-gather.3.cloned.1.call-update) | async-done | bytes 7602192 | tf_op jit(solution)/shard_map/all_gather | solution.py:300
  113.9 6.7 %shard_map.159 = bf16[8,144,256]{2,1,0:T(8,128)(2,1)} custom-call(s32[1,128]{1,0:T(1,128)} %fusion.col, bf16[128,1024]{1,0:T(8,128)(2,1)} %hidden.3, bf16[1024,3712]{1,0:T(8,128)(2,1)} %all-gather.3.cloned.1.call-done.weight), custom_call_target="tpu_custom_call" | custom-call | flops 2000000000 | bytes 6000000 | tf_op jit(solution)/shard_map/pallas_call | solution.py:237
  120.6 5.4 %all-to-all-start.3 = ((bf16[8,144,256]{2,1,0:T(8,128)(2,1)}), bf16[8,144,256]{2,1,0:T(8,128)(2,1)S(1)}, u32[]{:S(2)}, u32[]{:S(2)}) async-start(bf16[8,144,256]{2,1,0:T(8,128)(2,1)} %shard_map.159), calls=%async_computation.3 | async-start | bytes 1179648 | tf_op jit(solution)/shard_map/all_to_all | solution.py:350
  126.0 0.1 copy.17
  126.1 0.0 copy-start
  126.2 1.8 %slice.7.weight = bf16[1024,1024]{1,0:T(8,128)(2,1)S(1)} slice(bf16[1024,3712]{1,0:T(8,128)(2,1)} %all-gather.3.cloned.1.call-done.weight), slice={[0:1024], [2688:3712]} | slice | bytes 4194304 | tf_op jit(solution)/shard_map/slice | solution.py:354
  128.0 8.1 %all-to-all-done.3.parts = bf16[8,144,256]{2,1,0:T(8,128)(2,1)S(1)} async-done(((bf16[8,144,256]{2,1,0:T(8,128)(2,1)}), bf16[8,144,256]{2,1,0:T(8,128)(2,1)S(1)}, u32[]{:S(2)}, u32[]{:S(2)}) %all-to-all-start.3) | async-done | bytes 589856 | tf_op jit(solution)/shard_map/all_to_all | solution.py:350
  136.1 0.0 copy-done
  136.1 1.6 %shard_map.160 = (bf16[8,128,128]{2,1,0:T(8,128)(2,1)}, f32[128,128]{1,0:T(8,128)S(1)}, f32[1,128]{1,0:T(1,128)}) custom-call(bf16[8,144,256]{2,1,0:T(8,128)(2,1)S(1)} %all-to-all-done.3.parts, f32[128,128]{1,0:T(8,128)S(1)} %copy-done, f32[1,128]{1,0:T(1,128)S(1)} %copy-done.1, bf16[2,128,128]{2,1,0:T(8,128)(2,1)S(1)} %bitcast.20, ...), custom_call_target="tpu_custom_call" | custom-call | flops 10000000 | bytes 1000000 | tf_op jit(solution)/shard_map/pallas_call | solution.py:53
  137.7 4.3 %all-to-all-start.4 = ((bf16[8,128,128]{2,1,0:T(8,128)(2,1)}), bf16[8,128,128]{2,1,0:T(8,128)(2,1)S(1)}, u32[]{:S(2)}, u32[]{:S(2)}) async-start(bf16[8,128,128]{2,1,0:T(8,128)(2,1)} %get-tuple-element.34), calls=%async_computation.4 | async-start | bytes 524288 | tf_op jit(solution)/shard_map/all_to_all | solution.py:358
  142.0 2.6 %shard_map.162 = (f32[256,384]{1,0:T(8,128)}, f32[64,1152]{1,0:T(8,128)}, f32[128,256]{1,0:T(8,128)}, f32[64,128]{1,0:T(8,128)}) custom-call(s32[1]{0:T(128)} %bitcast.1.ch, bf16[128,256]{1,0:T(8,128)(2,1)} %copy-done.3, bf16[128,256]{1,0:T(8,128)(2,1)} %get-tuple-element.36.feat, bf16[128,256]{1,0:T(8,128)(2,1)} %get-tuple-element.37.dz1, ...), custom_call_target="tpu_custom_call" | custom-call | flops 10000000 | bytes 1000000 | tf_op jit(solution)/shard_map/pallas_call | solution.py:53
  144.5 3.9 %all-to-all-done.4.parts = bf16[8,128,128]{2,1,0:T(8,128)(2,1)S(1)} async-done(((bf16[8,128,128]{2,1,0:T(8,128)(2,1)}), bf16[8,128,128]{2,1,0:T(8,128)(2,1)S(1)}, u32[]{:S(2)}, u32[]{:S(2)}) %all-to-all-start.4) | async-done | bytes 262176 | tf_op jit(solution)/shard_map/all_to_all | solution.py:358
  148.5 0.7 shard_map.161
  (12 shorter events, 0.1 us)
Async XLA Ops:
  7.2 106.7 %all-gather.3.cloned.1.call-start = ((), (), s32[]{:S(2)}) async-start(), calls=%async_computation.5 | async-start | bytes 7720960 | tf_op jit(solution)/shard_map/all_gather | solution.py:300
  39.7 16.2 %copy-start.3 = (bf16[128,256]{1,0:T(8,128)(2,1)}, bf16[128,256]{1,0:T(8,128)(2,1)S(1)}, u32[]{:S(2)}) copy-start(bf16[128,256]{1,0:T(8,128)(2,1)S(1)} %reshape.44.got) | copy-start | bytes 196612
  59.8 32.1 %copy-start.5 = (s32[128]{0:T(128)S(1)}, s32[128]{0:T(128)}, u32[]{:S(2)}) copy-start(s32[128]{0:T(128)} %param.21) | copy-start | bytes 1540
  59.8 32.1 %copy-start.6 = (s32[128]{0:T(128)S(1)}, s32[128]{0:T(128)}, u32[]{:S(2)}) copy-start(s32[128]{0:T(128)} %param.20) | copy-start | bytes 1540
  59.8 21.8 %all-to-all-start.1 = ((bf16[8,128,640]{2,1,0:T(8,128)(2,1)}), bf16[8,128,640]{2,1,0:T(8,128)(2,1)S(1)}, u32[]{:S(2)}, u32[]{:S(2)}) async-start(bf16[8,128,640]{2,1,0:T(8,128)(2,1)} %get-tuple-element.26), calls=%async_computation.1 | async-start | bytes 2621440 | tf_op jit(solution)/shard_map/all_to_all | solution.py:324
  81.6 1.1 copy-start.2
  87.3 16.4 %all-to-all-start.2 = ((bf16[64,2,256]{2,1,0:T(2,128)(2,1)}), bf16[64,2,256]{2,1,0:T(2,128)(2,1)S(1)}, u32[]{:S(2)}, u32[]{:S(2)}) async-start(bf16[64,2,256]{2,1,0:T(2,128)(2,1)} %reshape.45), calls=%async_computation.2 | async-start | bytes 131072 | tf_op jit(solution)/shard_map/all_to_all | solution.py:331
  113.9 12.2 %copy-start.4 = (bf16[2,128,128]{2,1,0:T(8,128)(2,1)S(1)}, bf16[2,128,128]{2,1,0:T(8,128)(2,1)}, u32[]{:S(2)}) copy-start(bf16[2,128,128]{2,1,0:T(8,128)(2,1)} %param.12) | copy-start | bytes 196612
  120.6 15.5 %all-to-all-start.3 = ((bf16[8,144,256]{2,1,0:T(8,128)(2,1)}), bf16[8,144,256]{2,1,0:T(8,128)(2,1)S(1)}, u32[]{:S(2)}, u32[]{:S(2)}) async-start(bf16[8,144,256]{2,1,0:T(8,128)(2,1)} %shard_map.159), calls=%async_computation.3 | async-start | bytes 1179648 | tf_op jit(solution)/shard_map/all_to_all | solution.py:350
  126.1 9.9 %copy-start = (f32[128,128]{1,0:T(8,128)S(1)}, f32[128,128]{1,0:T(8,128)}, u32[]{:S(2)}) copy-start(f32[128,128]{1,0:T(8,128)} %get-tuple-element.31.back_t) | copy-start | bytes 196612
  126.2 9.9 %copy-start.1 = (f32[1,128]{1,0:T(1,128)S(1)}, f32[1,128]{1,0:T(1,128)}, u32[]{:S(2)}) copy-start(f32[1,128]{1,0:T(1,128)} %get-tuple-element.32.tail_loss) | copy-start | bytes 1540
  137.7 10.8 %all-to-all-start.4 = ((bf16[8,128,128]{2,1,0:T(8,128)(2,1)}), bf16[8,128,128]{2,1,0:T(8,128)(2,1)S(1)}, u32[]{:S(2)}, u32[]{:S(2)}) async-start(bf16[8,128,128]{2,1,0:T(8,128)(2,1)} %get-tuple-element.34), calls=%async_computation.4 | async-start | bytes 524288 | tf_op jit(solution)/shard_map/all_to_all | solution.py:358
Sparse Core Ops, SparseCore 0:
  11.6 102.2 all-gather.2

commit v4 on v3

--- a/solution.py
+++ b/solution.py
@@ -24,7 +24,7 @@
 W2 = 1152
 P1 = 256
 P2 = 64
-SROW = 16
+SROW = 8
 NEG = -1e30
 LIMIT = 24 * 2**20
 f32 = jnp.float32
@@ -226,8 +226,9 @@
         line = iota((SROW, 2 * T), 0)
         stats = jnp.zeros((SROW, 2 * T), f32)
         rows = parts3(stat[0:1, :]) + parts3(stat[1:2, :]) + parts3(stat[2:3, :])
-        for i, x in enumerate(rows):
-            stats = jnp.where(line == i, jnp.concatenate([x, x], axis=1), stats)
+        rows.append(jnp.zeros((1, T), f32))
+        for i in range(len(rows) // 2):
+            stats = jnp.where(line == i, jnp.concatenate(rows[2 * i : 2 * i + 2], axis=1), stats)
         for g in range(NCH):
             out[g, :NAR, :] = acc[g * NAR : (g + 1) * NAR, :].astype(bf16)
             out[g, NAR:, :] = stats.astype(bf16)
@@ -253,8 +254,8 @@
 def conv_kernel(parts, back_t, tail_loss, gates, weight, conv, grad, loss, taps):
     tops, totals, target = [], [], 0.0
     for g in range(NCH):
-        stats = parts[g, NAR:, :T].astype(f32)
-        s3 = [stats[i : i + 1] for i in range(9)]
+        stats = parts[g, NAR:, :].astype(f32)
+        s3 = [stats[i // 2 : i // 2 + 1, i % 2 * T : (i % 2 + 1) * T] for i in range(9)]
         tops.append(s3[0] + s3[1] + s3[2])
         totals.append(s3[3] + s3[4] + s3[5])
         target = target + (s3[6] + s3[7] + s3[8])

time: 157 us -> 156 us (level)
  no operation moved by 1% of the time
where the time goes in v4:
time: 156 us
  waiting for transfers between devices  48.6 us (31%)
  blocking collectives  44.2 us (28%)
  Pallas kernels  23.8 us (15%)
  starting transfers between devices  18.3 us (12%)
  between operations  14.1 us (9%)
  local copies, waits for them, and re-layouts  6.14 us (4%)
    all_to_all x1, blocking collectives, on_device(): lax.all_to_all(send.reshape(OWN, 2, NAR + 128), 'tok', split_axis=0, conc...  28 us
    all_to_all x1, waiting for transfers between devices, on_device(): parts = lax.all_to_all(part, 'ch', split_axis=0, concat_axis=0, tiled=True)  17.8 us
    pallas_call x8, Pallas kernels, call(): pl.pallas_call(kernel, out_shape=outs, in_specs=[VMEM] * len(args) if spe...  17.1 us
    all_gather x1, blocking collectives, on_device(): row_parts = lax.all_gather(got[:, :NAR], 'ch')  16.2 us
    all_to_all x1, waiting for transfers between devices, on_device(): lax.all_to_all(back.reshape(OWN, 2, NAR + 128), 'tok', split_axis=0, conc...  11.2 us
    all_gather x1, waiting for transfers between devices, on_device(): gathered = lax.all_gather(packed, 'tok', axis=0, tiled=True)  7.86 us
    all_to_all x1, waiting for transfers between devices, on_device(): lax.all_to_all(head, 'ch', split_axis=0, concat_axis=0, tiled=True)  7.75 us
    pallas_call x1, Pallas kernels, head_call(): pl.pallas_call(head_kernel, out_shape=jax.ShapeDtypeStruct((NCH, NAR + SR...  6.72 us
  transfers between devices with their start and end apart: 5, of which 5 were waited for; matrix products, arithmetic and copies ran while one was open for 4% of the time, Pallas kernels for 8%

profile of v4, /device:TPU:1, one launch (start us, length us, event | category | flops | bytes accessed | tf_op | source)
XLA Modules:
  0.0 155.7 jit_solution(4815994715068461124)
XLA Ops:
  7.2 0.0 all-gather.3.cloned.1.call-start
  7.2 1.6 %shard_map.154 = bf16[16,3712]{1,0:T(8,128)(2,1)} custom-call(bf16[16,2560]{1,0:T(8,128)(2,1)} %head.1, bf16[16,16]{1,0:T(8,128)(2,1)} %cluster.1, bf16[2,4,16,128]{3,2,1,0:T(8,128)(2,1)} %conv.1), custom_call_target="tpu_custom_call" | custom-call | flops 10000000 | bytes 1000000 | tf_op jit(solution)/shard_map/pallas_call | solution.py:53
  8.8 0.0 all-gather.3.cloned.1.call-update
  8.8 2.0 %shard_map.155 = (bf16[128,256]{1,0:T(8,128)(2,1)}, bf16[128,128]{1,0:T(8,128)(2,1)}) custom-call(s32[1]{0:T(128)} %bitcast.1.ch, s32[1,128]{1,0:T(1,128)} %bitcast.31, s32[1,128]{1,0:T(1,128)} %bitcast.30, bf16[128,1024]{1,0:T(8,128)(2,1)} %hidden.3), custom_call_target="tpu_custom_call" | custom-call | flops 10000000 | bytes 1000000 | tf_op jit(solution)/shard_map/pallas_call | solution.py:53
  10.8 0.9 reshape.43
  11.7 28.0 %all_to_all.25 = bf16[64,2,256]{2,1,0:T(2,128)(2,1)S(1)} all-to-all(bf16[64,2,256]{2,1,0:T(2,128)(2,1)S(1)} %reshape.43), channel_id=1, replica_groups=mesh['tok'=64,'ch'=8] {'tok'}, dimensions={0} | all-to-all | bytes 131072 | tf_op jit(solution)/shard_map/all_to_all | solution.py:312
  39.7 0.0 copy-start.3
  39.7 16.2 %all-gather = bf16[1024,128]{1,0:T(8,128)(2,1)} all-gather(bf16[128,128]{1,0:T(8,128)(2,1)S(1)} %slice.8), channel_id=2, replica_groups=mesh['tok'=64,'ch'=8] {'ch'}, dimensions={0}, use_global_device_ids=true | all-gather | bytes 294912 | tf_op jit(solution)/shard_map/all_gather | solution.py:313
  55.9 3.9 %shard_map.156 = (bf16[128,256]{1,0:T(8,128)(2,1)}, bf16[8,128,640]{2,1,0:T(8,128)(2,1)}) custom-call(s32[1]{0:T(128)} %bitcast.1.ch, bf16[128,256]{1,0:T(8,128)(2,1)} %copy-done.3, bf16[8,128,128]{2,1,0:T(8,128)(2,1)} %bitcast.23, bf16[1024,256]{1,0:T(8,128)(2,1)} %bitcast.21, bf16[64,1024]{1,0:T(8,128)(2,1)} %bitcast.28, bf16[256,384]{1,0:T(8,128)(2,1)} %bitcast.24, ...), custom_call_target="tpu_custom_call" | custom-call | flops 10000000 | bytes 1000000 | tf_op jit(solution)/shard_map/pallas_call | solution.py:53
  59.8 4.0 %all-to-all-start.1 = ((bf16[8,128,640]{2,1,0:T(8,128)(2,1)}), bf16[8,128,640]{2,1,0:T(8,128)(2,1)S(1)}, u32[]{:S(2)}, u32[]{:S(2)}) async-start(bf16[8,128,640]{2,1,0:T(8,128)(2,1)} %get-tuple-element.26), calls=%async_computation.1 | async-start | bytes 2621440 | tf_op jit(solution)/shard_map/all_to_all | solution.py:325
  63.8 17.8 %all-to-all-done.1.parts = bf16[8,128,640]{2,1,0:T(8,128)(2,1)S(1)} async-done(((bf16[8,128,640]{2,1,0:T(8,128)(2,1)}), bf16[8,128,640]{2,1,0:T(8,128)(2,1)S(1)}, u32[]{:S(2)}, u32[]{:S(2)}) %all-to-all-start.1) | async-done | bytes 1310752 | tf_op jit(solution)/shard_map/all_to_all | solution.py:325
  81.6 1.1 copy-done.2
  82.7 3.1 %shard_map.157 = (bf16[128,256]{1,0:T(8,128)(2,1)}, bf16[128,256]{1,0:T(8,128)(2,1)}, f32[128,128]{1,0:T(8,128)}, bf16[128,256]{1,0:T(8,128)(2,1)}) custom-call(s32[1]{0:T(128)} %bitcast.1.ch, bf16[128,256]{1,0:T(8,128)(2,1)} %copy-done.3, bf16[8,128,640]{2,1,0:T(8,128)(2,1)} %copy-done.2, bf16[1024,256]{1,0:T(8,128)(2,1)} %bitcast.22, bf16[64,1024]{1,0:T(8,128)(2,1)} %bitcast.29), custom_call_target="tpu_custom_call" | custom-call | flops 10000000 | bytes 1000000 | tf_op jit(solution)/shard_map/pallas_call | solution.py:53
  85.8 1.5 reshape.45
  87.3 4.6 %all-to-all-start.2 = ((bf16[64,2,256]{2,1,0:T(2,128)(2,1)}), bf16[64,2,256]{2,1,0:T(2,128)(2,1)S(1)}, u32[]{:S(2)}, u32[]{:S(2)}) async-start(bf16[64,2,256]{2,1,0:T(2,128)(2,1)} %reshape.45), calls=%async_computation.2 | async-start | bytes 131072 | tf_op jit(solution)/shard_map/all_to_all | solution.py:332
  91.9 0.5 fusion.col
  92.5 11.2 %all-to-all-done.2 = bf16[64,2,256]{2,1,0:T(2,128)(2,1)S(1)} async-done(((bf16[64,2,256]{2,1,0:T(2,128)(2,1)}), bf16[64,2,256]{2,1,0:T(2,128)(2,1)S(1)}, u32[]{:S(2)}, u32[]{:S(2)}) %all-to-all-start.2) | async-done | bytes 65568 | tf_op jit(solution)/shard_map/all_to_all | solution.py:332
  103.7 0.7 reshape.46.got
  104.3 1.7 %shard_map.158 = (f32[128,128]{1,0:T(8,128)}, f32[1,128]{1,0:T(1,128)}) custom-call(bf16[128,256]{1,0:T(8,128)(2,1)} %reshape.46.got, bf16[128,128]{1,0:T(8,128)(2,1)} %get-tuple-element.28.pick), custom_call_target="tpu_custom_call" | custom-call | flops 10000000 | bytes 1000000 | tf_op jit(solution)/shard_map/pallas_call | solution.py:53
  106.0 7.9 %all-gather.3.cloned.1.call-done.weight = bf16[1024,3712]{1,0:T(8,128)(2,1)} async-done(((bf16[16,3712]{1,0:T(8,128)(2,1)}), bf16[1024,3712]{1,0:T(8,128)(2,1)}) %all-gather.3.cloned.1.call-update) | async-done | bytes 7602192 | tf_op jit(solution)/shard_map/all_gather | solution.py:301
  113.9 6.7 %shard_map.159 = bf16[8,136,256]{2,1,0:T(8,128)(2,1)} custom-call(s32[1,128]{1,0:T(1,128)} %fusion.col, bf16[128,1024]{1,0:T(8,128)(2,1)} %hidden.3, bf16[1024,3712]{1,0:T(8,128)(2,1)} %all-gather.3.cloned.1.call-done.weight), custom_call_target="tpu_custom_call" | custom-call | flops 2000000000 | bytes 6000000 | tf_op jit(solution)/shard_map/pallas_call | solution.py:238
  120.6 5.4 %all-to-all-start.3 = ((bf16[8,136,256]{2,1,0:T(8,128)(2,1)}), bf16[8,136,256]{2,1,0:T(8,128)(2,1)S(1)}, u32[]{:S(2)}, u32[]{:S(2)}) async-start(bf16[8,136,256]{2,1,0:T(8,128)(2,1)} %shard_map.159), calls=%async_computation.3 | async-start | bytes 1114112 | tf_op jit(solution)/shard_map/all_to_all | solution.py:351
  126.0 0.1 copy.17
  126.1 0.0 copy-start
  126.1 1.8 %slice.7.weight = bf16[1024,1024]{1,0:T(8,128)(2,1)S(1)} slice(bf16[1024,3712]{1,0:T(8,128)(2,1)} %all-gather.3.cloned.1.call-done.weight), slice={[0:1024], [2688:3712]} | slice | bytes 4194304 | tf_op jit(solution)/shard_map/slice | solution.py:355
  127.9 7.8 %all-to-all-done.3.parts = bf16[8,136,256]{2,1,0:T(8,128)(2,1)S(1)} async-done(((bf16[8,136,256]{2,1,0:T(8,128)(2,1)}), bf16[8,136,256]{2,1,0:T(8,128)(2,1)S(1)}, u32[]{:S(2)}, u32[]{:S(2)}) %all-to-all-start.3) | async-done | bytes 557088 | tf_op jit(solution)/shard_map/all_to_all | solution.py:351
  135.7 0.0 copy-done.1
  135.7 1.6 %shard_map.160 = (bf16[8,128,128]{2,1,0:T(8,128)(2,1)}, f32[128,128]{1,0:T(8,128)S(1)}, f32[1,128]{1,0:T(1,128)}) custom-call(bf16[8,136,256]{2,1,0:T(8,128)(2,1)S(1)} %all-to-all-done.3.parts, f32[128,128]{1,0:T(8,128)S(1)} %copy-done, f32[1,128]{1,0:T(1,128)S(1)} %copy-done.1, bf16[2,128,128]{2,1,0:T(8,128)(2,1)S(1)} %bitcast.20, ...), custom_call_target="tpu_custom_call" | custom-call | flops 10000000 | bytes 1000000 | tf_op jit(solution)/shard_map/pallas_call | solution.py:53
  137.3 4.3 %all-to-all-start.4 = ((bf16[8,128,128]{2,1,0:T(8,128)(2,1)}), bf16[8,128,128]{2,1,0:T(8,128)(2,1)S(1)}, u32[]{:S(2)}, u32[]{:S(2)}) async-start(bf16[8,128,128]{2,1,0:T(8,128)(2,1)} %get-tuple-element.34), calls=%async_computation.4 | async-start | bytes 524288 | tf_op jit(solution)/shard_map/all_to_all | solution.py:359
  141.6 2.6 %shard_map.162 = (f32[256,384]{1,0:T(8,128)}, f32[64,1152]{1,0:T(8,128)}, f32[128,256]{1,0:T(8,128)}, f32[64,128]{1,0:T(8,128)}) custom-call(s32[1]{0:T(128)} %bitcast.1.ch, bf16[128,256]{1,0:T(8,128)(2,1)} %copy-done.3, bf16[128,256]{1,0:T(8,128)(2,1)} %get-tuple-element.36.feat, bf16[128,256]{1,0:T(8,128)(2,1)} %get-tuple-element.37.dz1, ...), custom_call_target="tpu_custom_call" | custom-call | flops 10000000 | bytes 1000000 | tf_op jit(solution)/shard_map/pallas_call | solution.py:53
  144.2 3.9 %all-to-all-done.4.parts = bf16[8,128,128]{2,1,0:T(8,128)(2,1)S(1)} async-done(((bf16[8,128,128]{2,1,0:T(8,128)(2,1)}), bf16[8,128,128]{2,1,0:T(8,128)(2,1)S(1)}, u32[]{:S(2)}, u32[]{:S(2)}) %all-to-all-start.4) | async-done | bytes 262176 | tf_op jit(solution)/shard_map/all_to_all | solution.py:359
  148.1 0.7 shard_map.161
  (12 shorter events, 0.1 us)
Async XLA Ops:
  7.2 106.7 %all-gather.3.cloned.1.call-start = ((), (), s32[]{:S(2)}) async-start(), calls=%async_computation.5 | async-start | bytes 7720960 | tf_op jit(solution)/shard_map/all_gather | solution.py:301
  39.7 16.2 %copy-start.3 = (bf16[128,256]{1,0:T(8,128)(2,1)}, bf16[128,256]{1,0:T(8,128)(2,1)S(1)}, u32[]{:S(2)}) copy-start(bf16[128,256]{1,0:T(8,128)(2,1)S(1)} %reshape.44.got) | copy-start | bytes 196612
  59.8 32.1 %copy-start.5 = (s32[128]{0:T(128)S(1)}, s32[128]{0:T(128)}, u32[]{:S(2)}) copy-start(s32[128]{0:T(128)} %param.21) | copy-start | bytes 1540
  59.8 32.1 %copy-start.6 = (s32[128]{0:T(128)S(1)}, s32[128]{0:T(128)}, u32[]{:S(2)}) copy-start(s32[128]{0:T(128)} %param.20) | copy-start | bytes 1540
  59.8 21.8 %all-to-all-start.1 = ((bf16[8,128,640]{2,1,0:T(8,128)(2,1)}), bf16[8,128,640]{2,1,0:T(8,128)(2,1)S(1)}, u32[]{:S(2)}, u32[]{:S(2)}) async-start(bf16[8,128,640]{2,1,0:T(8,128)(2,1)} %get-tuple-element.26), calls=%async_computation.1 | async-start | bytes 2621440 | tf_op jit(solution)/shard_map/all_to_all | solution.py:325
  81.6 1.1 copy-start.2
  87.3 16.4 %all-to-all-start.2 = ((bf16[64,2,256]{2,1,0:T(2,128)(2,1)}), bf16[64,2,256]{2,1,0:T(2,128)(2,1)S(1)}, u32[]{:S(2)}, u32[]{:S(2)}) async-start(bf16[64,2,256]{2,1,0:T(2,128)(2,1)} %reshape.45), calls=%async_computation.2 | async-start | bytes 131072 | tf_op jit(solution)/shard_map/all_to_all | solution.py:332
  113.9 12.1 %copy-start.4 = (bf16[2,128,128]{2,1,0:T(8,128)(2,1)S(1)}, bf16[2,128,128]{2,1,0:T(8,128)(2,1)}, u32[]{:S(2)}) copy-start(bf16[2,128,128]{2,1,0:T(8,128)(2,1)} %param.12) | copy-start | bytes 196612
  120.6 15.1 %all-to-all-start.3 = ((bf16[8,136,256]{2,1,0:T(8,128)(2,1)}), bf16[8,136,256]{2,1,0:T(8,128)(2,1)S(1)}, u32[]{:S(2)}, u32[]{:S(2)}) async-start(bf16[8,136,256]{2,1,0:T(8,128)(2,1)} %shard_map.159), calls=%async_computation.3 | async-start | bytes 1114112 | tf_op jit(solution)/shard_map/all_to_all | solution.py:351
  126.1 9.6 %copy-start = (f32[128,128]{1,0:T(8,128)S(1)}, f32[128,128]{1,0:T(8,128)}, u32[]{:S(2)}) copy-start(f32[128,128]{1,0:T(8,128)} %get-tuple-element.31.back_t) | copy-start | bytes 196612
  126.1 9.6 %copy-start.1 = (f32[1,128]{1,0:T(1,128)S(1)}, f32[1,128]{1,0:T(1,128)}, u32[]{:S(2)}) copy-start(f32[1,128]{1,0:T(1,128)} %get-tuple-element.32.tail_loss) | copy-start | bytes 1540
  137.3 10.8 %all-to-all-start.4 = ((bf16[8,128,128]{2,1,0:T(8,128)(2,1)}), bf16[8,128,128]{2,1,0:T(8,128)(2,1)S(1)}, u32[]{:S(2)}, u32[]{:S(2)}) async-start(bf16[8,128,128]{2,1,0:T(8,128)(2,1)} %get-tuple-element.34), calls=%async_computation.4 | async-start | bytes 524288 | tf_op jit(solution)/shard_map/all_to_all | solution.py:359
Sparse Core Ops, SparseCore 0:
  11.6 102.2 all-gather.2

commit v5 on v4

--- a/solution.py
+++ b/solution.py
@@ -18,7 +18,8 @@
 CW = 16
 GW = HW + CW
 HP = 2688
-BLK = 896
+BLK = 1280
+TAIL = 128
 CONV = 2 * K * NAR
 W1 = 384
 W2 = 1152
@@ -195,7 +196,7 @@
     loss[...] = terms[0:1] + terms[1:2] + terms[2:3]
 
 
-def head_kernel(col, hidden, weight, out, acc, stat):
+def head_kernel(col, hidden, weight, clusters, out, acc, stat):
     step = pl.program_id(0)
 
     @pl.when(step == 0)
@@ -205,24 +206,29 @@
         stat[1:2, :] = jnp.zeros((1, T), f32)
         stat[2:3, :] = jnp.zeros((1, T), f32)
 
-    logits = dot(hidden[...], weight[...]).T
-    index = iota((BLK, T), 0) + step * BLK
-    logits = jnp.where(index < GW, logits, NEG)
-    old = stat[0:1, :]
-    top = jnp.maximum(old, jnp.max(logits, axis=0, keepdims=True))
-    scale = jnp.exp(old - top)
-    terms = jnp.exp(logits - top)
-    hot = index == col[...]
-    stat[0:1, :] = top
-    stat[1:2, :] = stat[1:2, :] * scale + jnp.sum(terms, axis=0, keepdims=True)
-    stat[2:3, :] = stat[2:3, :] + jnp.sum(jnp.where(hot, logits, 0.0), axis=0, keepdims=True)
-    right = jnp.concatenate([jnp.where(hot, 0.0, terms), hot.astype(f32)], axis=1).astype(bf16)
-    new = dot(weight[...], right)
-    acc[:, :T] = acc[:, :T] * scale + new[:, :T]
-    acc[:, T:] = acc[:, T:] + new[:, T:]
+    def absorb(block, start, size):
+        logits = dot(hidden[...], block[...]).T
+        index = iota((size, T), 0) + start
+        if size == TAIL:
+            logits = jnp.where(index < GW, logits, NEG)
+        old = stat[0:1, :]
+        top = jnp.maximum(old, jnp.max(logits, axis=0, keepdims=True))
+        scale = jnp.exp(old - top)
+        terms = jnp.exp(logits - top)
+        hot = index == col[...]
+        stat[0:1, :] = top
+        stat[1:2, :] = stat[1:2, :] * scale + jnp.sum(terms, axis=0, keepdims=True)
+        stat[2:3, :] = stat[2:3, :] + jnp.sum(jnp.where(hot, logits, 0.0), axis=0, keepdims=True)
+        right = jnp.concatenate([jnp.where(hot, 0.0, terms), hot.astype(f32)], axis=1).astype(bf16)
+        new = dot(block[...], right)
+        acc[:, :T] = acc[:, :T] * scale + new[:, :T]
+        acc[:, T:] = acc[:, T:] + new[:, T:]
+
+    absorb(weight, step * BLK, BLK)
 
     @pl.when(step == pl.num_programs(0) - 1)
     def _():
+        absorb(clusters, HW, TAIL)
         line = iota((SROW, 2 * T), 0)
         stats = jnp.zeros((SROW, 2 * T), f32)
         rows = parts3(stat[0:1, :]) + parts3(stat[1:2, :]) + parts3(stat[2:3, :])
@@ -238,17 +244,18 @@
     return pl.pallas_call(
         head_kernel,
         out_shape=jax.ShapeDtypeStruct((NCH, NAR + SROW, 2 * T), bf16),
-        grid=(HP // BLK,),
+        grid=(HW // BLK,),
         in_specs=[
             pl.BlockSpec((1, T), lambda i: (0, 0)),
             pl.BlockSpec((T, D), lambda i: (0, 0)),
             pl.BlockSpec((D, BLK), lambda i: (0, i)),
+            pl.BlockSpec((D, TAIL), lambda i: (0, HW // TAIL)),
         ],
         out_specs=pl.BlockSpec((NCH, NAR + SROW, 2 * T), lambda i: (0, 0, 0)),
         scratch_shapes=[pltpu.VMEM((D, 2 * T), f32), pltpu.VMEM((8, T), f32)],
         compiler_params=pltpu.CompilerParams(dimension_semantics=("arbitrary",)),
         cost_estimate=pl.CostEstimate(flops=2 * 10**9, bytes_accessed=6 * 10**6, transcendentals=0),
-    )(col, hidden, weight)
+    )(col, hidden, weight, weight)
 
 
 def conv_kernel(parts, back_t, tail_loss, gates, weight, conv, grad, loss, taps):

time: 156 us -> 156 us (level)
  no operation moved by 1% of the time
where the time goes in v5:
time: 156 us
  waiting for transfers between devices  48.6 us (31%)
  blocking collectives  44.2 us (28%)
  Pallas kernels  23.8 us (15%)
  starting transfers between devices  18.4 us (12%)
  between operations  14.1 us (9%)
  local copies, waits for them, and re-layouts  6.14 us (4%)
    all_to_all x1, blocking collectives, on_device(): lax.all_to_all(send.reshape(OWN, 2, NAR + 128), 'tok', split_axis=0, conc...  28 us
    all_to_all x1, waiting for transfers between devices, on_device(): parts = lax.all_to_all(part, 'ch', split_axis=0, concat_axis=0, tiled=True)  17.8 us
    pallas_call x8, Pallas kernels, call(): pl.pallas_call(kernel, out_shape=outs, in_specs=[VMEM] * len(args) if spe...  17.1 us
    all_gather x1, blocking collectives, on_device(): row_parts = lax.all_gather(got[:, :NAR], 'ch')  16.2 us
    all_to_all x1, waiting for transfers between devices, on_device(): lax.all_to_all(back.reshape(OWN, 2, NAR + 128), 'tok', split_axis=0, conc...  11.2 us
    all_gather x1, waiting for transfers between devices, on_device(): gathered = lax.all_gather(packed, 'tok', axis=0, tiled=True)  7.86 us
    all_to_all x1, waiting for transfers between devices, on_device(): lax.all_to_all(head, 'ch', split_axis=0, concat_axis=0, tiled=True)  7.75 us
    pallas_call x1, Pallas kernels, head_call(): pl.pallas_call(head_kernel, out_shape=jax.ShapeDtypeStruct((NCH, NAR + SR...  6.71 us
  transfers between devices with their start and end apart: 5, of which 5 were waited for; matrix products, arithmetic and copies ran while one was open for 4% of the time, Pallas kernels for 8%

profile of v5, /device:TPU:1, one launch (start us, length us, event | category | flops | bytes accessed | tf_op | source)
XLA Modules:
  0.0 155.7 jit_solution(2862310497669862526)
XLA Ops:
  7.2 0.0 all-gather.3.cloned.1.call-start
  7.2 1.6 %shard_map.154 = bf16[16,3712]{1,0:T(8,128)(2,1)} custom-call(bf16[16,2560]{1,0:T(8,128)(2,1)} %head.1, bf16[16,16]{1,0:T(8,128)(2,1)} %cluster.1, bf16[2,4,16,128]{3,2,1,0:T(8,128)(2,1)} %conv.1), custom_call_target="tpu_custom_call" | custom-call | flops 10000000 | bytes 1000000 | tf_op jit(solution)/shard_map/pallas_call | solution.py:54
  8.8 0.0 all-gather.3.cloned.1.call-update
  8.8 2.0 %shard_map.155 = (bf16[128,256]{1,0:T(8,128)(2,1)}, bf16[128,128]{1,0:T(8,128)(2,1)}) custom-call(s32[1]{0:T(128)} %bitcast.1.ch, s32[1,128]{1,0:T(1,128)} %bitcast.31, s32[1,128]{1,0:T(1,128)} %bitcast.30, bf16[128,1024]{1,0:T(8,128)(2,1)} %hidden.3), custom_call_target="tpu_custom_call" | custom-call | flops 10000000 | bytes 1000000 | tf_op jit(solution)/shard_map/pallas_call | solution.py:54
  10.8 0.9 reshape.43
  11.7 28.0 %all_to_all.25 = bf16[64,2,256]{2,1,0:T(2,128)(2,1)S(1)} all-to-all(bf16[64,2,256]{2,1,0:T(2,128)(2,1)S(1)} %reshape.43), channel_id=1, replica_groups=mesh['tok'=64,'ch'=8] {'tok'}, dimensions={0} | all-to-all | bytes 131072 | tf_op jit(solution)/shard_map/all_to_all | solution.py:319
  39.7 16.2 %all-gather = bf16[1024,128]{1,0:T(8,128)(2,1)} all-gather(bf16[128,128]{1,0:T(8,128)(2,1)S(1)} %slice.8), channel_id=2, replica_groups=mesh['tok'=64,'ch'=8] {'ch'}, dimensions={0}, use_global_device_ids=true | all-gather | bytes 294912 | tf_op jit(solution)/shard_map/all_gather | solution.py:320
  55.9 3.9 %shard_map.156 = (bf16[128,256]{1,0:T(8,128)(2,1)}, bf16[8,128,640]{2,1,0:T(8,128)(2,1)}) custom-call(s32[1]{0:T(128)} %bitcast.1.ch, bf16[128,256]{1,0:T(8,128)(2,1)} %copy-done.3, bf16[8,128,128]{2,1,0:T(8,128)(2,1)} %bitcast.23, bf16[1024,256]{1,0:T(8,128)(2,1)} %bitcast.21, bf16[64,1024]{1,0:T(8,128)(2,1)} %bitcast.28, bf16[256,384]{1,0:T(8,128)(2,1)} %bitcast.24, ...), custom_call_target="tpu_custom_call" | custom-call | flops 10000000 | bytes 1000000 | tf_op jit(solution)/shard_map/pallas_call | solution.py:54
  59.8 4.0 %all-to-all-start.1 = ((bf16[8,128,640]{2,1,0:T(8,128)(2,1)}), bf16[8,128,640]{2,1,0:T(8,128)(2,1)S(1)}, u32[]{:S(2)}, u32[]{:S(2)}) async-start(bf16[8,128,640]{2,1,0:T(8,128)(2,1)} %get-tuple-element.26), calls=%async_computation.1 | async-start | bytes 2621440 | tf_op jit(solution)/shard_map/all_to_all | solution.py:332
  63.8 17.8 %all-to-all-done.1.parts = bf16[8,128,640]{2,1,0:T(8,128)(2,1)S(1)} async-done(((bf16[8,128,640]{2,1,0:T(8,128)(2,1)}), bf16[8,128,640]{2,1,0:T(8,128)(2,1)S(1)}, u32[]{:S(2)}, u32[]{:S(2)}) %all-to-all-start.1) | async-done | bytes 1310752 | tf_op jit(solution)/shard_map/all_to_all | solution.py:332
  81.6 1.1 copy-done.2
  82.7 3.1 %shard_map.157 = (bf16[128,256]{1,0:T(8,128)(2,1)}, bf16[128,256]{1,0:T(8,128)(2,1)}, f32[128,128]{1,0:T(8,128)}, bf16[128,256]{1,0:T(8,128)(2,1)}) custom-call(s32[1]{0:T(128)} %bitcast.1.ch, bf16[128,256]{1,0:T(8,128)(2,1)} %copy-done.3, bf16[8,128,640]{2,1,0:T(8,128)(2,1)} %copy-done.2, bf16[1024,256]{1,0:T(8,128)(2,1)} %bitcast.22, bf16[64,1024]{1,0:T(8,128)(2,1)} %bitcast.29), custom_call_target="tpu_custom_call" | custom-call | flops 10000000 | bytes 1000000 | tf_op jit(solution)/shard_map/pallas_call | solution.py:54
  85.8 1.5 reshape.45
  87.3 4.6 %all-to-all-start.2 = ((bf16[64,2,256]{2,1,0:T(2,128)(2,1)}), bf16[64,2,256]{2,1,0:T(2,128)(2,1)S(1)}, u32[]{:S(2)}, u32[]{:S(2)}) async-start(bf16[64,2,256]{2,1,0:T(2,128)(2,1)} %reshape.45), calls=%async_computation.2 | async-start | bytes 131072 | tf_op jit(solution)/shard_map/all_to_all | solution.py:339
  91.9 0.5 fusion.col
  92.5 11.2 %all-to-all-done.2 = bf16[64,2,256]{2,1,0:T(2,128)(2,1)S(1)} async-done(((bf16[64,2,256]{2,1,0:T(2,128)(2,1)}), bf16[64,2,256]{2,1,0:T(2,128)(2,1)S(1)}, u32[]{:S(2)}, u32[]{:S(2)}) %all-to-all-start.2) | async-done | bytes 65568 | tf_op jit(solution)/shard_map/all_to_all | solution.py:339
  103.7 0.7 reshape.46.got
  104.3 1.7 %shard_map.158 = (f32[128,128]{1,0:T(8,128)}, f32[1,128]{1,0:T(1,128)}) custom-call(bf16[128,256]{1,0:T(8,128)(2,1)} %reshape.46.got, bf16[128,128]{1,0:T(8,128)(2,1)} %get-tuple-element.28.pick), custom_call_target="tpu_custom_call" | custom-call | flops 10000000 | bytes 1000000 | tf_op jit(solution)/shard_map/pallas_call | solution.py:54
  106.0 7.9 %all-gather.3.cloned.1.call-done.weight.clusters = bf16[1024,3712]{1,0:T(8,128)(2,1)} async-done(((bf16[16,3712]{1,0:T(8,128)(2,1)}), bf16[1024,3712]{1,0:T(8,128)(2,1)}) %all-gather.3.cloned.1.call-update) | async-done | bytes 7602192 | tf_op jit(solution)/shard_map/all_gather | solution.py:308
  113.9 6.7 %shard_map.159 = bf16[8,136,256]{2,1,0:T(8,128)(2,1)} custom-call(s32[1,128]{1,0:T(1,128)} %fusion.col, bf16[128,1024]{1,0:T(8,128)(2,1)} %hidden.3, bf16[1024,3712]{1,0:T(8,128)(2,1)} %all-gather.3.cloned.1.call-done.weight.clusters, bf16[1024,3712]{1,0:T(8,128)(2,1)} %all-gather.3.cloned.1.call-done.weight.clusters), custom_call_target="tpu_custom_call" | custom-call | flops 2000000000 | bytes 6000000 | tf_op jit(solution)/shard_map/pallas_call | solution.py:244
  120.6 5.4 %all-to-all-start.3 = ((bf16[8,136,256]{2,1,0:T(8,128)(2,1)}), bf16[8,136,256]{2,1,0:T(8,128)(2,1)S(1)}, u32[]{:S(2)}, u32[]{:S(2)}) async-start(bf16[8,136,256]{2,1,0:T(8,128)(2,1)} %shard_map.159), calls=%async_computation.3 | async-start | bytes 1114112 | tf_op jit(solution)/shard_map/all_to_all | solution.py:358
  126.0 0.1 copy.17
  126.1 0.0 copy-start
  126.1 0.0 copy-start.1
  126.1 1.8 %slice.7.weight = bf16[1024,1024]{1,0:T(8,128)(2,1)S(1)} slice(bf16[1024,3712]{1,0:T(8,128)(2,1)} %all-gather.3.cloned.1.call-done.weight.clusters), slice={[0:1024], [2688:3712]} | slice | bytes 4194304 | tf_op jit(solution)/shard_map/slice | solution.py:362
  127.9 7.8 %all-to-all-done.3.parts = bf16[8,136,256]{2,1,0:T(8,128)(2,1)S(1)} async-done(((bf16[8,136,256]{2,1,0:T(8,128)(2,1)}), bf16[8,136,256]{2,1,0:T(8,128)(2,1)S(1)}, u32[]{:S(2)}, u32[]{:S(2)}) %all-to-all-start.3) | async-done | bytes 557088 | tf_op jit(solution)/shard_map/all_to_all | solution.py:358
  135.7 0.0 copy-done
  135.7 1.6 %shard_map.160 = (bf16[8,128,128]{2,1,0:T(8,128)(2,1)}, f32[128,128]{1,0:T(8,128)S(1)}, f32[1,128]{1,0:T(1,128)}) custom-call(bf16[8,136,256]{2,1,0:T(8,128)(2,1)S(1)} %all-to-all-done.3.parts, f32[128,128]{1,0:T(8,128)S(1)} %copy-done, f32[1,128]{1,0:T(1,128)S(1)} %copy-done.1, bf16[2,128,128]{2,1,0:T(8,128)(2,1)S(1)} %bitcast.20, ...), custom_call_target="tpu_custom_call" | custom-call | flops 10000000 | bytes 1000000 | tf_op jit(solution)/shard_map/pallas_call | solution.py:54
  137.3 4.3 %all-to-all-start.4 = ((bf16[8,128,128]{2,1,0:T(8,128)(2,1)}), bf16[8,128,128]{2,1,0:T(8,128)(2,1)S(1)}, u32[]{:S(2)}, u32[]{:S(2)}) async-start(bf16[8,128,128]{2,1,0:T(8,128)(2,1)} %get-tuple-element.34), calls=%async_computation.4 | async-start | bytes 524288 | tf_op jit(solution)/shard_map/all_to_all | solution.py:366
  141.6 2.6 %shard_map.162 = (f32[256,384]{1,0:T(8,128)}, f32[64,1152]{1,0:T(8,128)}, f32[128,256]{1,0:T(8,128)}, f32[64,128]{1,0:T(8,128)}) custom-call(s32[1]{0:T(128)} %bitcast.1.ch, bf16[128,256]{1,0:T(8,128)(2,1)} %copy-done.3, bf16[128,256]{1,0:T(8,128)(2,1)} %get-tuple-element.36.feat, bf16[128,256]{1,0:T(8,128)(2,1)} %get-tuple-element.37.dz1, ...), custom_call_target="tpu_custom_call" | custom-call | flops 10000000 | bytes 1000000 | tf_op jit(solution)/shard_map/pallas_call | solution.py:54
  144.2 3.9 %all-to-all-done.4.parts = bf16[8,128,128]{2,1,0:T(8,128)(2,1)S(1)} async-done(((bf16[8,128,128]{2,1,0:T(8,128)(2,1)}), bf16[8,128,128]{2,1,0:T(8,128)(2,1)S(1)}, u32[]{:S(2)}, u32[]{:S(2)}) %all-to-all-start.4) | async-done | bytes 262176 | tf_op jit(solution)/shard_map/all_to_all | solution.py:366
  148.1 0.7 shard_map.161
  (12 shorter events, 0.1 us)
Async XLA Ops:
  7.2 106.7 %all-gather.3.cloned.1.call-start = ((), (), s32[]{:S(2)}) async-start(), calls=%async_computation.5 | async-start | bytes 7720960 | tf_op jit(solution)/shard_map/all_gather | solution.py:308
  39.7 16.2 %copy-start.3 = (bf16[128,256]{1,0:T(8,128)(2,1)}, bf16[128,256]{1,0:T(8,128)(2,1)S(1)}, u32[]{:S(2)}) copy-start(bf16[128,256]{1,0:T(8,128)(2,1)S(1)} %reshape.44.got) | copy-start | bytes 196612
  59.8 32.1 %copy-start.5 = (s32[128]{0:T(128)S(1)}, s32[128]{0:T(128)}, u32[]{:S(2)}) copy-start(s32[128]{0:T(128)} %param.21) | copy-start | bytes 1540
  59.8 32.1 %copy-start.6 = (s32[128]{0:T(128)S(1)}, s32[128]{0:T(128)}, u32[]{:S(2)}) copy-start(s32[128]{0:T(128)} %param.20) | copy-start | bytes 1540
  59.8 21.8 %all-to-all-start.1 = ((bf16[8,128,640]{2,1,0:T(8,128)(2,1)}), bf16[8,128,640]{2,1,0:T(8,128)(2,1)S(1)}, u32[]{:S(2)}, u32[]{:S(2)}) async-start(bf16[8,128,640]{2,1,0:T(8,128)(2,1)} %get-tuple-element.26), calls=%async_computation.1 | async-start | bytes 2621440 | tf_op jit(solution)/shard_map/all_to_all | solution.py:332
  81.6 1.1 copy-start.2
  87.3 16.4 %all-to-all-start.2 = ((bf16[64,2,256]{2,1,0:T(2,128)(2,1)}), bf16[64,2,256]{2,1,0:T(2,128)(2,1)S(1)}, u32[]{:S(2)}, u32[]{:S(2)}) async-start(bf16[64,2,256]{2,1,0:T(2,128)(2,1)} %reshape.45), calls=%async_computation.2 | async-start | bytes 131072 | tf_op jit(solution)/shard_map/all_to_all | solution.py:339
  113.9 12.1 %copy-start.4 = (bf16[2,128,128]{2,1,0:T(8,128)(2,1)S(1)}, bf16[2,128,128]{2,1,0:T(8,128)(2,1)}, u32[]{:S(2)}) copy-start(bf16[2,128,128]{2,1,0:T(8,128)(2,1)} %param.12) | copy-start | bytes 196612
  120.6 15.1 %all-to-all-start.3 = ((bf16[8,136,256]{2,1,0:T(8,128)(2,1)}), bf16[8,136,256]{2,1,0:T(8,128)(2,1)S(1)}, u32[]{:S(2)}, u32[]{:S(2)}) async-start(bf16[8,136,256]{2,1,0:T(8,128)(2,1)} %shard_map.159), calls=%async_computation.3 | async-start | bytes 1114112 | tf_op jit(solution)/shard_map/all_to_all | solution.py:358
  126.1 9.6 %copy-start = (f32[128,128]{1,0:T(8,128)S(1)}, f32[128,128]{1,0:T(8,128)}, u32[]{:S(2)}) copy-start(f32[128,128]{1,0:T(8,128)} %get-tuple-element.31.back_t) | copy-start | bytes 196612
  126.1 9.6 %copy-start.1 = (f32[1,128]{1,0:T(1,128)S(1)}, f32[1,128]{1,0:T(1,128)}, u32[]{:S(2)}) copy-start(f32[1,128]{1,0:T(1,128)} %get-tuple-element.32.tail_loss) | copy-start | bytes 1540
  137.3 10.8 %all-to-all-start.4 = ((bf16[8,128,128]{2,1,0:T(8,128)(2,1)}), bf16[8,128,128]{2,1,0:T(8,128)(2,1)S(1)}, u32[]{:S(2)}, u32[]{:S(2)}) async-start(bf16[8,128,128]{2,1,0:T(8,128)(2,1)} %get-tuple-element.34), calls=%async_computation.4 | async-start | bytes 524288 | tf_op jit(solution)/shard_map/all_to_all | solution.py:366
Sparse Core Ops, SparseCore 0:
  11.6 102.2 all-gather.2
